TPU v7x, 32 devices: a whole 2x2x4 slice. The times are simulated.
32 devices in a mesh: groups: 1, pairs: 4 (over z), chol: 4 (over y, x), walk: 2 (over core).
Axes of the slice: x: 2, y: 2, z: 4, core: 2. Of those that a mesh axis runs over, the one named last changes fastest.
Arguments:
- chol_vectors: bfloat16 [512, 768, 768], P(('groups', 'walk'), 'pairs', 'chol'), as said below
- trial_orbitals: float32 [768, 256], P('groups'), as said below
- walkers: float32 [16, 768, 256], P(('groups', 'pairs', 'chol'), None, 'walk'), as said below
- field_noise: float32 [1, 16, 512], P('groups', None, 'walk'), may hold values from -6 to 6
Outputs:
- propagated: float32 [16, 768, 256], P(('groups', 'pairs', 'chol'), None, 'walk')
- force_bias: float32 [1, 16, 512], P('groups', None, 'walk')
Inputs may be any that keep to these rules, and one draw needn't show every extreme that they name: chol_vectors[g, p, q] = chol_vectors[g, q, p] for every g. The columns of trial_orbitals are linearly independent. `walkers`: every walker's intersection with trial_orbitals is far from singular.
All inputs are finite; a program needn't handle non-finite values.
Results may differ from a plain program's by a relative error of at most 0.0029.
Values may be sent and summed in bfloat16 or wider, within the bound.
No kernel may reach another device: no remote copies, remote signals or barrier semaphores. Data moves between devices by JAX's collectives and lax.ppermute only.
A program may use at most 64 MiB of HBM per device.

v0:
```python
import functools

import jax
import jax.numpy as jnp
from jax import lax
from jax.experimental import pallas as pl
from jax.experimental.pallas import tpu as pltpu
from jax.sharding import PartitionSpec as P

TERMS = 6


root_step = 0.05
highest = lax.Precision.HIGHEST
GROUP = 16
LANES = 128
f32 = jnp.float32
bf16 = jnp.bfloat16


def swapped(value, axis, apart):
    mask = 2**apart
    pairs = [(source, source ^ mask) for source in range(lax.axis_size(axis))]
    return lax.ppermute(value, axis, pairs)


def solve_normal(factor, right_side):
    middle = lax.linalg.triangular_solve(factor, right_side, left_side=True, lower=True)
    return lax.linalg.triangular_solve(factor, middle, left_side=True, lower=True, transpose_a=True)


def green_blocks(walker_full, trial_orbitals, trial_part, row_groups, col_groups):
    owner_walkers, orbital_count, electron_count = walker_full.shape
    intersection = jnp.einsum("nm,wnk->wmk", trial_orbitals, walker_full, precision=highest)
    normal = jnp.einsum("wmk,wml->wkl", intersection, intersection, precision=highest)
    factor = jnp.linalg.cholesky(normal)
    rotated = jnp.einsum("wmk,cbm->wkcb", intersection, trial_part, precision=highest)
    chosen_cols = rotated.shape[2] * rotated.shape[3]
    solved = solve_normal(factor, rotated.reshape(owner_walkers, electron_count, chosen_cols))
    slab_rows = orbital_count // row_groups
    block_cols = chosen_cols // col_groups
    shaped = solved.reshape(owner_walkers, electron_count, col_groups, block_cols)
    walker_rows = walker_full.reshape(owner_walkers, row_groups, slab_rows, electron_count)
    blocks = jnp.einsum("wiak,wkcb->icwab", walker_rows, shaped, precision=highest)
    return blocks.astype(jnp.bfloat16).reshape(
        row_groups * col_groups, owner_walkers, slab_rows * block_cols
    )


def shards(chol_vectors, trial_orbitals, walkers, field_noise):
    held_vectors, slab_rows, slab_cols = chol_vectors.shape
    owner_walkers = walkers.shape[0]
    orbital_count = walkers.shape[1]
    electron_count = trial_orbitals.shape[1]
    row_groups = lax.axis_size("pairs")
    col_groups = lax.axis_size("chol")
    core_count = lax.axis_size("walk")
    core_index = lax.axis_index("walk")
    core_cols = slab_cols // core_count
    owner_count = row_groups * col_groups
    walker_total = owner_count * owner_walkers
    flat_vectors = chol_vectors.reshape(held_vectors, slab_rows * slab_cols)
    trial_split = trial_orbitals.reshape(col_groups, core_count, core_cols, electron_count)
    trial_part = lax.dynamic_index_in_dim(trial_split, core_index, 1, keepdims=False)
    walker_full = lax.all_gather(walkers, "walk", axis=2, tiled=True)
    outgoing = green_blocks(walker_full, trial_orbitals, trial_part, row_groups, col_groups)
    sectioned = outgoing.reshape(row_groups, col_groups, owner_walkers, slab_rows * core_cols)
    arrived = lax.all_to_all(
        lax.all_to_all(sectioned, "pairs", split_axis=0, concat_axis=0, tiled=True),
        "chol",
        split_axis=1,
        concat_axis=1,
        tiled=True,
    )
    arrived = arrived.reshape(walker_total, slab_rows, core_cols)
    partial_bias = jnp.einsum(
        "wab,gab->wg",
        lax.all_gather(arrived, "walk", axis=2, tiled=True),
        chol_vectors,
        preferred_element_type=jnp.float32,
    )
    force_bias = lax.psum(partial_bias, ("pairs", "chol"))
    bias_steps = [force_bias]
    shifted = field_noise[0] + root_step * force_bias
    shifted_high = lax.optimization_barrier(shifted.astype(jnp.bfloat16))
    shifted_low = (shifted - shifted_high.astype(jnp.float32)).astype(jnp.bfloat16)
    stacked = jnp.stack([shifted_high, shifted_low])
    both_parts = lax.dot_general(
        stacked, flat_vectors, (((2,), (0,)), ((), ())), preferred_element_type=jnp.float32
    )
    potential = both_parts[0] + both_parts[1]
    blocks_out = potential.reshape(owner_count, owner_walkers, slab_rows * slab_cols)
    received = lax.all_to_all(
        blocks_out, ("pairs", "chol"), split_axis=0, concat_axis=0, tiled=True
    )
    partner = swapped(received, "walk", 0)
    summed = (received + partner).reshape(
        row_groups, col_groups, owner_walkers, slab_rows, core_count, core_cols
    )
    matrix = jnp.transpose(summed, (2, 0, 3, 1, 4, 5)).reshape(
        owner_walkers, orbital_count, orbital_count
    )
    running_term = walkers
    running_sum = walkers
    for degree in range(1, TERMS):
        running_term = -(root_step / degree) * jnp.einsum(
            "wpq,wqm->wpm", matrix, running_term, precision=highest
        )
        running_sum = running_sum + running_term
    return (running_sum, jnp.stack(bias_steps))


def split_two(value):
    high = value.astype(bf16)
    return high, (value - high.astype(f32)).astype(bf16)


def dot_of(left, right, dims=(((1,), (0,)), ((), ())), precision=None):
    return lax.dot_general(left, right, dims, precision=precision, preferred_element_type=f32)


def dot_three(left, right, dims=(((1,), (0,)), ((), ()))):
    left_high, left_low = split_two(left)
    right_high, right_low = split_two(right)
    return (
        dot_of(left_high, right_high, dims)
        + dot_of(left_high, right_low, dims)
        + dot_of(left_low, right_high, dims)
    )


first_dims = (((0,), (0,)), ((), ()))
last_dims = (((1,), (1,)), ((), ()))


def eye_of(size):
    rows = lax.broadcasted_iota(jnp.int32, (size, size), 0)
    cols = lax.broadcasted_iota(jnp.int32, (size, size), 1)
    return (rows == cols).astype(f32)


def half_rolled(value):
    return pltpu.roll(value, LANES // 2, 1)


def tail_lanes(value):
    return lax.broadcasted_iota(jnp.int32, value.shape, 1) < LANES // 2


LOW_START = 5e-4
PAIRED_STEPS = 6
RESIDUAL_BOUND = 3e-3
MOST_STEPS = 60


def scales():
    low = LOW_START
    found = []
    for _ in range(PAIRED_STEPS + 1):
        scale = 2.0 / (1.0 + 2.0 * low - low * low)
        found.append(scale)
        low = 2.0 - scale
    return found


def green_body(core_ref, own_ref, other_ref, trial_ref, out_ref, inverse_ref, matrix_ref, *, row_groups, col_groups):
    orbital_count, electron_count = trial_ref.shape
    slab_rows = orbital_count // row_groups
    slab_cols = orbital_count // col_groups
    core = core_ref[0]
    half = slab_rows // 2
    walker = jnp.concatenate([own_ref[...], other_ref[...]], axis=1)
    trial = trial_ref[...]
    inter = dot_of(trial, walker, first_dims, highest)
    inverse_scale = 1.0 / jnp.max(jnp.abs(inter))
    inter = inter * inverse_scale
    matrix_ref[...] = inter
    turned = inter.T
    eye = eye_of(electron_count)
    normal = dot_three(turned, inter)
    both = dot_three(normal, jnp.concatenate([normal, turned], axis=1))
    square = both[:, :electron_count]
    step_scales = scales()
    largest = jnp.sqrt(jnp.sqrt(jnp.sum(square * square))) * 1.001
    alpha = (2.0 - LOW_START) / largest
    scale = step_scales[0]
    error = eye - (2.0 * scale * alpha) * normal + (scale * alpha * alpha) * square
    inverse = (scale * alpha) * (2.0 * turned - alpha * both[:, electron_count:])
    for scale in step_scales[1:]:
        both = dot_three(error, jnp.concatenate([error, inverse], axis=1))
        inverse = scale * (inverse + both[:, electron_count:])
        error = (1.0 - scale) * eye + scale * both[:, :electron_count]
    inverse_ref[...] = inverse

    def refine(carried):
        count, _ = carried
        current = inverse_ref[...]
        residual = eye_of(electron_count) - dot_of(current, matrix_ref[...], precision=highest)
        inverse_ref[...] = current + dot_three(residual, current)
        return count + 1, jnp.sum(residual * residual)

    lax.while_loop(
        lambda carried: jnp.logical_and(carried[0] < MOST_STEPS, carried[1] > RESIDUAL_BOUND**2),
        refine,
        (jnp.int32(0), jnp.float32(1e30)),
    )
    chosen = []
    for row in range(row_groups):
        start = pl.multiple_of(row * slab_rows + core * half, 8)
        chosen.append(
            jnp.concatenate(
                [own_ref[pl.ds(start, half), :], other_ref[pl.ds(start, half), :]], axis=1
            )
        )
    scaled = dot_three(jnp.concatenate(chosen, axis=0), inverse_ref[...]) * inverse_scale
    pieces = [trial_ref[slab_cols * c : slab_cols * c + LANES, :] for c in range(col_groups)]
    pieces += [trial_ref[slab_cols * c + LANES : slab_cols * (c + 1), :] for c in range(col_groups)]
    green = dot_three(scaled, jnp.concatenate(pieces, axis=0), last_dims)
    quarter = half // 2
    for row in range(row_groups):
        for col in range(col_groups):
            place = row * col_groups + col
            slab = green[row * half : (row + 1) * half]
            out_ref[place, 0:half, :] = slab[:, col * LANES : (col + 1) * LANES].astype(bf16)
            start = (col_groups + col // 2) * LANES
            top = slab[:quarter, start : start + LANES]
            bottom = slab[quarter:, start : start + LANES]
            if col % 2 == 0:
                packed = jnp.where(tail_lanes(top), top, half_rolled(bottom))
            else:
                packed = jnp.where(tail_lanes(top), half_rolled(top), bottom)
            out_ref[place, half : half + quarter, :] = packed.astype(bf16)


def bias_body(core_ref, own_ref, other_ref, vector_ref, out_ref, green_ref, sums_ref, *, slab_rows, slab_cols):
    step = pl.program_id(0)
    walker_total = own_ref.shape[0]
    block = vector_ref.shape[0]
    half = slab_rows // 2
    groups = half // GROUP
    wide = walker_total * GROUP

    @pl.when(step == 0)
    def _():
        core = core_ref[0]
        for source, place in ((own_ref, core), (other_ref, 1 - core)):
            for group in range(groups):
                main = source[:, group * GROUP : (group + 1) * GROUP, :].reshape(wide, LANES)
                start = half + (group % (groups // 2)) * GROUP
                tail = source[:, start : start + GROUP, :].reshape(wide, LANES)
                if group >= groups // 2:
                    tail = half_rolled(tail.astype(f32)).astype(bf16)
                green_ref[place * groups + group, :, 0:LANES] = main
                green_ref[place * groups + group, :, LANES:slab_cols] = tail[:, 0 : slab_cols - LANES]

    total = jnp.zeros((block * GROUP, wide), f32)
    for group in range(slab_rows // GROUP):
        chosen = vector_ref[:, group * GROUP : (group + 1) * GROUP, :]
        total = total + dot_of(chosen.reshape(block * GROUP, slab_cols), green_ref[group], last_dims)
    rows = lax.broadcasted_iota(jnp.int32, total.shape, 0) % GROUP
    cols = lax.broadcasted_iota(jnp.int32, total.shape, 1) % GROUP
    kept = jnp.where(rows == cols, total, 0.0)
    start = pl.multiple_of(step * block, block)
    sums_ref[pl.ds(start, block), :] = kept.reshape(block, GROUP, wide).sum(axis=1)

    @pl.when(step == pl.num_programs(0) - 1)
    def _():
        owner = lax.broadcasted_iota(jnp.int32, (walker_total, wide), 0)
        place = lax.broadcasted_iota(jnp.int32, (walker_total, wide), 1) // GROUP
        bias = dot_of((owner == place).astype(f32), sums_ref[...], last_dims, highest)
        for device in range(out_ref.shape[0]):
            out_ref[device] = bias


def potential_body(core_ref, parts_ref, noise_ref, vector_ref, bias_ref, keep_ref, send_ref, weights_ref, mixed_ref, total_ref, *, slab_rows, slab_cols):
    step = pl.program_id(0)
    walker_total, held = noise_ref.shape
    block = vector_ref.shape[0]
    wide = walker_total * GROUP
    half = slab_rows // 2
    groups = half // GROUP

    @pl.when(step == 0)
    def _():
        bias = parts_ref[0]
        for device in range(1, parts_ref.shape[0]):
            bias = bias + parts_ref[device]
        bias_ref[...] = bias
        shifted = noise_ref[...] + root_step * bias
        spread = jnp.broadcast_to(shifted[:, None, :], (walker_total, GROUP, held)).reshape(wide, held)
        high, low = split_two(spread)
        weights_ref[0:wide, :] = high
        weights_ref[wide : 2 * wide, :] = low

    source = lax.broadcasted_iota(jnp.int32, (held, block * GROUP), 0)
    target = lax.broadcasted_iota(jnp.int32, (held, block * GROUP), 1)
    chooser = (source == step * block + target // GROUP).astype(bf16)
    mixed = dot_of(weights_ref[...], chooser)
    rows = lax.broadcasted_iota(jnp.int32, mixed.shape, 0) % GROUP
    cols = lax.broadcasted_iota(jnp.int32, mixed.shape, 1) % GROUP
    mixed_ref[...] = jnp.where(rows == cols, mixed, 0.0).astype(bf16)
    for group in range(slab_rows // GROUP):
        chosen = vector_ref[:, group * GROUP : (group + 1) * GROUP, :]
        both = dot_of(mixed_ref[...], chosen.reshape(block * GROUP, slab_cols))
        added = both[:wide] + both[wide:]

        @pl.when(step == 0)
        def _():
            total_ref[group] = added

        @pl.when(step > 0)
        def _():
            total_ref[group] = total_ref[group] + added

    @pl.when(step == pl.num_programs(0) - 1)
    def _():
        core = core_ref[0]
        shape = (walker_total, GROUP, LANES)
        for target_ref, place in ((keep_ref, core), (send_ref, 1 - core)):
            for group in range(groups):
                value = total_ref[place * groups + group]
                target_ref[:, group * GROUP : (group + 1) * GROUP, :] = value[:, :LANES].reshape(shape)
                if group < groups // 2:
                    paired = total_ref[place * groups + group + groups // 2]
                    tail = jnp.concatenate([value[:, LANES:], paired[:, LANES:]], axis=1)
                    start = half + group * GROUP
                    target_ref[:, start : start + GROUP, :] = tail.reshape(shape)


def series_body(core_ref, own_ref, other_ref, walker_ref, out_ref, matrix_ref, *, row_groups, col_groups):
    orbital_count = walker_ref.shape[0]
    slab_rows = orbital_count // row_groups
    slab_cols = orbital_count // col_groups
    half = slab_rows // 2
    quarter = half // 2
    core = core_ref[0]
    for source, place in ((own_ref, core), (other_ref, 1 - core)):
        for row in range(row_groups):
            start = pl.multiple_of(row * slab_rows + place * half, GROUP)
            for col in range(col_groups):
                index = row * col_groups + col
                matrix_ref[pl.ds(start, half), col * LANES : (col + 1) * LANES] = source[index, 0:half, :]
            for col in range(0, col_groups, 2):
                index = row * col_groups + col
                even = source[index, half : half + quarter, :].astype(f32)
                odd = source[index + 1, half : half + quarter, :].astype(f32)
                top = jnp.where(tail_lanes(even), even, half_rolled(odd))
                bottom = jnp.where(tail_lanes(even), half_rolled(even), odd)
                lane = (col_groups + col // 2) * LANES
                joined = jnp.concatenate([top, bottom], axis=0).astype(bf16)
                matrix_ref[pl.ds(start, half), lane : lane + LANES] = joined

    term = walker_ref[...]
    total = term
    width = term.shape[1]
    for degree in range(1, TERMS):
        order = [term[slab_cols * c : slab_cols * c + LANES] for c in range(col_groups)]
        order += [term[slab_cols * c + LANES : slab_cols * (c + 1)] for c in range(col_groups)]
        high, low = split_two(jnp.concatenate(order, axis=0))
        both = dot_of(matrix_ref[...], jnp.concatenate([high, low], axis=1))
        term = (-root_step / degree) * (both[:, :width] + both[:, width:])
        total = total + term
    out_ref[...] = total


smem = pl.BlockSpec(memory_space=pltpu.SMEM)
vmem = pl.BlockSpec(memory_space=pltpu.VMEM)
BLOCK = 32


def fast_shards(chol_vectors, trial_orbitals, walkers, field_noise):
    held, slab_rows, slab_cols = chol_vectors.shape
    orbital_count, electron_count = trial_orbitals.shape
    row_groups = lax.axis_size("pairs")
    col_groups = lax.axis_size("chol")
    owners = row_groups * col_groups
    half = slab_rows // 2
    dense = half + half // 2
    wide = owners * GROUP
    core = lax.axis_index("walk").astype(jnp.int32).reshape(1)
    own = walkers[0]
    other = swapped(own, "walk", 0)
    outgoing = pl.pallas_call(
        functools.partial(green_body, row_groups=row_groups, col_groups=col_groups),
        out_shape=jax.ShapeDtypeStruct((owners, dense, LANES), bf16),
        in_specs=[smem, vmem, vmem, vmem],
        out_specs=vmem,
        scratch_shapes=[pltpu.VMEM((electron_count, electron_count), f32)] * 2,
        name="green",
    )(core, own, other, trial_orbitals)
    axes = ("pairs", "chol")
    arrived = lax.all_to_all(outgoing, axes, split_axis=0, concat_axis=0, tiled=True)
    arrived_other = swapped(arrived, "walk", 0)
    blocks = pl.BlockSpec((BLOCK, slab_rows, slab_cols), lambda step: (step, 0, 0))
    spread = pl.pallas_call(
        functools.partial(bias_body, slab_rows=slab_rows, slab_cols=slab_cols),
        grid=(held // BLOCK,),
        out_shape=jax.ShapeDtypeStruct((owners, owners, held), f32),
        in_specs=[smem, vmem, vmem, blocks],
        out_specs=vmem,
        scratch_shapes=[
            pltpu.VMEM((slab_rows // GROUP, wide, slab_cols), bf16),
            pltpu.VMEM((held, wide), f32),
        ],
        name="bias",
    )(core, arrived, arrived_other, chol_vectors)
    parts = lax.all_to_all(spread, axes, split_axis=0, concat_axis=0, tiled=True)
    force_bias, keep, send = pl.pallas_call(
        functools.partial(potential_body, slab_rows=slab_rows, slab_cols=slab_cols),
        grid=(held // BLOCK,),
        out_shape=(
            jax.ShapeDtypeStruct((owners, held), f32),
            jax.ShapeDtypeStruct((owners, dense, LANES), f32),
            jax.ShapeDtypeStruct((owners, dense, LANES), f32),
        ),
        in_specs=[smem, vmem, vmem, blocks],
        out_specs=(vmem, vmem, vmem),
        scratch_shapes=[
            pltpu.VMEM((2 * wide, held), bf16),
            pltpu.VMEM((2 * wide, BLOCK * GROUP), bf16),
            pltpu.VMEM((slab_rows // GROUP, wide, slab_cols), f32),
        ],
        name="potential",
    )(core, parts, field_noise[0], chol_vectors)
    summed = (keep + swapped(send, "walk", 0)).astype(bf16)
    received = lax.all_to_all(summed, axes, split_axis=0, concat_axis=0, tiled=True)
    received_other = swapped(received, "walk", 0)
    propagated = pl.pallas_call(
        functools.partial(series_body, row_groups=row_groups, col_groups=col_groups),
        out_shape=jax.ShapeDtypeStruct(own.shape, f32),
        in_specs=[smem, vmem, vmem, vmem],
        out_specs=vmem,
        scratch_shapes=[pltpu.VMEM((orbital_count, orbital_count), bf16)],
        name="series",
    )(core, received, received_other, own)
    return propagated[None], force_bias[None]


def packable(chol_vectors, trial_orbitals, walkers, field_noise):
    held, slab_rows, slab_cols = chol_vectors.shape
    owners = lax.axis_size("pairs") * lax.axis_size("chol")
    return (
        walkers.shape[0] == 1
        and owners * GROUP <= 512
        and lax.axis_size("walk") == 2
        and lax.axis_size("chol") % 2 == 0
        and slab_cols == LANES + LANES // 2
        and slab_rows % (4 * GROUP) == 0
        and held % BLOCK == 0
        and trial_orbitals.shape[1] % 256 == 0
        and field_noise.shape[0] == 1
    )


def chosen_shards(*args):
    return fast_shards(*args) if packable(*args) else shards(*args)


def solution(mesh):
    placed = (
        P(("groups", "walk"), "pairs", "chol"),
        P("groups", None),
        P(("groups", "pairs", "chol"), None, "walk"),
        P("groups", None, "walk"),
    )
    return jax.shard_map(
        chosen_shards,
        mesh=mesh,
        in_specs=placed,
        out_specs=(P(("groups", "pairs", "chol"), None, "walk"), P("groups", None, "walk")),
        check_vma=False,
    )
```

profile of v0, /device:TPU:0, one launch (start us, length us, event | category | flops | bytes accessed | tf_op | source)
XLA Modules:
  0.0 186.1 jit_solution(13989518496517437392)
XLA Ops:
  0.6 0.6 collective-permute-start
  1.2 1.6 collective-permute-done.other_ref
  2.7 0.0 copy-start.4
  2.8 0.7 copy-done.4
  3.5 11.1 %green.1 = bf16[16,144,128]{2,1,0:T(8,128)(2,1)} custom-call(s32[1]{0:T(128)} %bitcast.core_ref, f32[768,128]{1,0:T(8,128)} %bitcast.6, f32[768,128]{1,0:T(8,128)} %copy-done.4, f32[768,256]{1,0:T(8,128)} %trial_ref.1), custom_call_target="tpu_custom_call" | custom-call | tf_op jit(solution)/shard_map/green/pallas_call | solution.py:383
  14.6 26.0 %all_to_all.15.own_ref = bf16[16,144,128]{2,1,0:T(8,128)(2,1)S(1)} all-to-all(bf16[16,144,128]{2,1,0:T(8,128)(2,1)} %green.1), channel_id=1, replica_groups=mesh['groups'=1,'pairs'=4,'chol'=4,'walk'=2] {'pairs','chol'}, dimensions={0} | all-to-all | bytes 1179648 | tf_op jit(solution)/shard_map/all_to_all | solution.py:392
  40.6 0.0 copy-start
  40.6 0.0 collective-permute-start.1
  40.6 34.3 %copy.6.vector_ref = bf16[256,192,192]{2,1,0:T(8,128)(2,1)} copy(bf16[256,192,192]{0,2,1:T(8,128)(2,1)} %param.4) | data formatting | bytes 37748736 | tf_op args[0]
  74.9 0.0 copy-done
  74.9 0.0 collective-permute-done.1.other_ref
  74.9 0.0 copy-start.2
  74.9 0.8 copy-done.2
  75.7 15.0 %bias.1 = f32[16,16,256]{2,1,0:T(8,128)} custom-call(s32[1]{0:T(128)} %bitcast.core_ref, bf16[16,144,128]{2,1,0:T(8,128)(2,1)} %copy-done, bf16[16,144,128]{2,1,0:T(8,128)(2,1)} %copy-done.2, bf16[256,192,192]{2,1,0:T(8,128)(2,1)} %copy.6.vector_ref), custom_call_target="tpu_custom_call" | custom-call | tf_op jit(solution)/shard_map/bias/pallas_call | solution.py:395
  90.7 14.8 %all_to_all.16.parts_ref = f32[16,16,256]{2,1,0:T(8,128)} all-to-all(f32[16,16,256]{2,1,0:T(8,128)} %bias.1), channel_id=1, replica_groups=mesh['groups'=1,'pairs'=4,'chol'=4,'walk'=2] {'pairs','chol'}, dimensions={0} | all-to-all | bytes 524288 | tf_op jit(solution)/shard_map/all_to_all | solution.py:407
  105.5 47.0 %potential.1 = (f32[16,256]{1,0:T(8,128)}, f32[16,144,128]{2,1,0:T(8,128)}, f32[16,144,128]{2,1,0:T(8,128)}) custom-call(s32[1]{0:T(128)} %bitcast.core_ref, f32[16,16,256]{2,1,0:T(8,128)} %all_to_all.16.parts_ref, f32[16,256]{1,0:T(8,128)} %bitcast.9, bf16[256,192,192]{2,1,0:T(8,128)(2,1)} %copy.6.vector_ref), custom_call_target="tpu_custom_call" | custom-call | tf_op jit(solution)/shard_map/potential/pallas_call | solution.py:408
  152.4 0.0 collective-permute-start.2
  152.4 3.1 %collective-permute-done.2 = f32[16,144,128]{2,1,0:T(8,128)S(1)} collective-permute-done((f32[16,144,128]{2,1,0:T(8,128)}, f32[16,144,128]{2,1,0:T(8,128)S(1)}, u32[]{:S(2)}, u32[]{:S(2)}) %collective-permute-start.2) | collective-permute-done | bytes 1179680 | tf_op jit(solution)/shard_map/ppermute | solution.py:24
  155.5 1.4 add_convert_fusion
  156.9 21.1 %all_to_all.17.own_ref = bf16[16,144,128]{2,1,0:T(8,128)(2,1)S(1)} all-to-all(bf16[16,144,128]{2,1,0:T(8,128)(2,1)S(1)} %add_convert_fusion), channel_id=1, replica_groups=mesh['groups'=1,'pairs'=4,'chol'=4,'walk'=2] {'pairs','chol'}, dimensions={0} | all-to-all | bytes 1179648 | tf_op jit(solution)/shard_map/all_to_all | solution.py:426
  178.0 0.0 copy-start.1
  178.0 0.0 collective-permute-start.3
  178.0 2.0 %collective-permute-done.3.other_ref = bf16[16,144,128]{2,1,0:T(8,128)(2,1)S(1)} collective-permute-done((bf16[16,144,128]{2,1,0:T(8,128)(2,1)S(1)}, bf16[16,144,128]{2,1,0:T(8,128)(2,1)S(1)}, u32[]{:S(2)}, u32[]{:S(2)}) %collective-permute-start.3) | collective-permute-done | bytes 589856 | tf_op jit(solution)/shard_map/ppermute | solution.py:24
  180.0 0.0 copy-done.1
  180.0 0.0 copy-start.3
  180.0 0.8 copy-done.3
  180.8 5.3 %series.1 = f32[768,128]{1,0:T(8,128)} custom-call(s32[1]{0:T(128)} %bitcast.core_ref, bf16[16,144,128]{2,1,0:T(8,128)(2,1)} %copy-done.1, bf16[16,144,128]{2,1,0:T(8,128)(2,1)} %copy-done.3, f32[768,128]{1,0:T(8,128)} %bitcast.7), custom_call_target="tpu_custom_call" | custom-call | tf_op jit(solution)/shard_map/series/pallas_call | solution.py:428
Async XLA Ops:
  0.6 2.1 %collective-permute-start = (f32[768,128]{1,0:T(8,128)}, f32[768,128]{1,0:T(8,128)S(1)}, u32[]{:S(2)}, u32[]{:S(2)}) collective-permute-start(f32[768,128]{1,0:T(8,128)} %bitcast.5), channel_id=1, source_target_pairs={{0,1},{1,0},{2,3},{3,2},{4,5},{5,4},{6,7},{7,6},{8,9},{9,8},{10,11... | collective-permute-start | bytes 1179656 | tf_op jit(solution)/shard_map/ppermute | solution.py:24
  2.7 0.7 copy-start.4
  40.6 34.3 %copy-start = (bf16[16,144,128]{2,1,0:T(8,128)(2,1)}, bf16[16,144,128]{2,1,0:T(8,128)(2,1)S(1)}, u32[]{:S(2)}) copy-start(bf16[16,144,128]{2,1,0:T(8,128)(2,1)S(1)} %all_to_all.15.own_ref) | copy-start | bytes 1769476
  40.6 34.3 %collective-permute-start.1 = (bf16[16,144,128]{2,1,0:T(8,128)(2,1)S(1)}, bf16[16,144,128]{2,1,0:T(8,128)(2,1)S(1)}, u32[]{:S(2)}, u32[]{:S(2)}) collective-permute-start(bf16[16,144,128]{2,1,0:T(8,128)(2,1)S(1)} %all_to_all.15.own_ref), channel_id=1, source_target_pairs={{0,1},{1,0},{2,3},{3,2},{4,5},{5,4},{6,7},{7,6},{8,9},{9,8},{10,11... | collective-permute-start | bytes 1769480 | tf_op jit(solution)/shard_map/ppermute | solution.py:24
  74.9 0.8 copy-start.2
  152.4 3.1 %collective-permute-start.2 = (f32[16,144,128]{2,1,0:T(8,128)}, f32[16,144,128]{2,1,0:T(8,128)S(1)}, u32[]{:S(2)}, u32[]{:S(2)}) collective-permute-start(f32[16,144,128]{2,1,0:T(8,128)} %get-tuple-element.6), channel_id=1, source_target_pairs={{0,1},{1,0},{2,3},{3,2},{4,5},{5,4},{6,7},{7,6},{8,9},{9,8},{10,11... | collective-permute-start | bytes 3538952 | tf_op jit(solution)/shard_map/ppermute | solution.py:24
  178.0 2.0 %copy-start.1 = (bf16[16,144,128]{2,1,0:T(8,128)(2,1)}, bf16[16,144,128]{2,1,0:T(8,128)(2,1)S(1)}, u32[]{:S(2)}) copy-start(bf16[16,144,128]{2,1,0:T(8,128)(2,1)S(1)} %all_to_all.17.own_ref) | copy-start | bytes 1769476
  178.0 2.0 %collective-permute-start.3 = (bf16[16,144,128]{2,1,0:T(8,128)(2,1)S(1)}, bf16[16,144,128]{2,1,0:T(8,128)(2,1)S(1)}, u32[]{:S(2)}, u32[]{:S(2)}) collective-permute-start(bf16[16,144,128]{2,1,0:T(8,128)(2,1)S(1)} %all_to_all.17.own_ref), channel_id=1, source_target_pairs={{0,1},{1,0},{2,3},{3,2},{4,5},{5,4},{6,7},{7,6},{8,9},{9,8},{10,11... | collective-permute-start | bytes 1769480 | tf_op jit(solution)/shard_map/ppermute | solution.py:24
  180.0 0.8 copy-start.3
where the time goes:
time: 187 us; the launch traced here: 186 us
  Pallas kernels  78.3 us (42%)
  blocking collectives  61.8 us (33%)
  local copies, waits for them, and re-layouts  36.7 us (20%)
  waiting for transfers between devices  6.62 us (4%)
    pallas_call x1, Pallas kernels, fast_shards(): pl.pallas_call(functools.partial(potential_body, slab_rows=slab_rows, sla...  47 us
    unnamed x11, local copies, waits for them, and re-layouts  36.7 us
    all_to_all x1, blocking collectives, fast_shards(): lax.all_to_all(outgoing, axes, split_axis=0, concat_axis=0, tiled=True)  26 us
    all_to_all x1, blocking collectives, fast_shards(): lax.all_to_all(summed, axes, split_axis=0, concat_axis=0, tiled=True)  21.1 us
    pallas_call x1, Pallas kernels, fast_shards(): pl.pallas_call(functools.partial(bias_body, slab_rows=slab_rows, slab_col...  15 us
    all_to_all x1, blocking collectives, fast_shards(): lax.all_to_all(spread, axes, split_axis=0, concat_axis=0, tiled=True)  14.8 us
    pallas_call x1, Pallas kernels, fast_shards(): pl.pallas_call(functools.partial(green_body, row_groups=row_groups, col_g...  11.1 us
    ppermute x4, waiting for transfers between devices, swapped(): return lax.ppermute(value, axis, pairs)  6.62 us
  transfers between devices with their start and end apart: 4, of which 3 were waited for; matrix products, arithmetic and copies ran while one was open for 18% of the time, Pallas kernels for 0%

commit v1 on v0

--- a/solution.py
+++ b/solution.py
@@ -223,8 +223,9 @@
             slab = green[row * half : (row + 1) * half]
             out_ref[place, 0:half, :] = slab[:, col * LANES : (col + 1) * LANES].astype(bf16)
             start = (col_groups + col // 2) * LANES
-            top = slab[:quarter, start : start + LANES]
-            bottom = slab[quarter:, start : start + LANES]
+            tails = slab[:, start : start + LANES].reshape(-1, 2, GROUP // 2, LANES)
+            top = tails[:, 0].reshape(quarter, LANES)
+            bottom = tails[:, 1].reshape(quarter, LANES)
             if col % 2 == 0:
                 packed = jnp.where(tail_lanes(top), top, half_rolled(bottom))
             else:
@@ -232,53 +233,43 @@
             out_ref[place, half : half + quarter, :] = packed.astype(bf16)
 
 
-def bias_body(core_ref, own_ref, other_ref, vector_ref, out_ref, green_ref, sums_ref, *, slab_rows, slab_cols):
+def packed_rows(vector_ref, group):
+    chosen = vector_ref[group * GROUP : (group + 1) * GROUP]
+    pieces = [chosen[row, :LANES] for row in range(GROUP)]
+    for row in range(GROUP // 2):
+        pieces += [chosen[row, LANES:], chosen[row + GROUP // 2, LANES:]]
+    return jnp.concatenate(pieces, axis=0)
+
+
+def bias_body(place_ref, green_ref, vector_ref, before_ref, out_ref, turned_ref, total_ref):
     step = pl.program_id(0)
-    walker_total = own_ref.shape[0]
-    block = vector_ref.shape[0]
-    half = slab_rows // 2
-    groups = half // GROUP
-    wide = walker_total * GROUP
+    groups = vector_ref.shape[0] // GROUP
+    half = pl.num_programs(0) * groups * GROUP
 
     @pl.when(step == 0)
     def _():
-        core = core_ref[0]
-        for source, place in ((own_ref, core), (other_ref, 1 - core)):
-            for group in range(groups):
-                main = source[:, group * GROUP : (group + 1) * GROUP, :].reshape(wide, LANES)
-                start = half + (group % (groups // 2)) * GROUP
-                tail = source[:, start : start + GROUP, :].reshape(wide, LANES)
-                if group >= groups // 2:
-                    tail = half_rolled(tail.astype(f32)).astype(bf16)
-                green_ref[place * groups + group, :, 0:LANES] = main
-                green_ref[place * groups + group, :, LANES:slab_cols] = tail[:, 0 : slab_cols - LANES]
-
-    total = jnp.zeros((block * GROUP, wide), f32)
-    for group in range(slab_rows // GROUP):
-        chosen = vector_ref[:, group * GROUP : (group + 1) * GROUP, :]
-        total = total + dot_of(chosen.reshape(block * GROUP, slab_cols), green_ref[group], last_dims)
-    rows = lax.broadcasted_iota(jnp.int32, total.shape, 0) % GROUP
-    cols = lax.broadcasted_iota(jnp.int32, total.shape, 1) % GROUP
-    kept = jnp.where(rows == cols, total, 0.0)
-    start = pl.multiple_of(step * block, block)
-    sums_ref[pl.ds(start, block), :] = kept.reshape(block, GROUP, wide).sum(axis=1)
+        turned_ref[...] = jnp.swapaxes(green_ref[...].astype(f32), 0, 1).astype(bf16)
+        total_ref[...] = before_ref[...]
+
+    total = total_ref[...]
+    for group in range(groups):
+        index = step * groups + group
+        pieces = [turned_ref[index * GROUP + row] for row in range(GROUP)]
+        pieces += [turned_ref[half + index * (GROUP // 2) + row] for row in range(GROUP // 2)]
+        total = total + dot_of(jnp.concatenate(pieces, axis=1), packed_rows(vector_ref, group))
+    total_ref[...] = total
 
     @pl.when(step == pl.num_programs(0) - 1)
     def _():
-        owner = lax.broadcasted_iota(jnp.int32, (walker_total, wide), 0)
-        place = lax.broadcasted_iota(jnp.int32, (walker_total, wide), 1) // GROUP
-        bias = dot_of((owner == place).astype(f32), sums_ref[...], last_dims, highest)
         for device in range(out_ref.shape[0]):
-            out_ref[device] = bias
-
-
-def potential_body(core_ref, parts_ref, noise_ref, vector_ref, bias_ref, keep_ref, send_ref, weights_ref, mixed_ref, total_ref, *, slab_rows, slab_cols):
+            out_ref[device] = total_ref[...]
+
+
+def potential_body(place_ref, parts_ref, noise_ref, vector_ref, bias_ref, out_ref, weights_ref):
     step = pl.program_id(0)
-    walker_total, held = noise_ref.shape
-    block = vector_ref.shape[0]
-    wide = walker_total * GROUP
-    half = slab_rows // 2
-    groups = half // GROUP
+    walker_total = noise_ref.shape[0]
+    groups = vector_ref.shape[0] // GROUP
+    half = pl.num_programs(0) * groups * GROUP
 
     @pl.when(step == 0)
     def _():
@@ -286,45 +277,18 @@
         for device in range(1, parts_ref.shape[0]):
             bias = bias + parts_ref[device]
         bias_ref[...] = bias
-        shifted = noise_ref[...] + root_step * bias
-        spread = jnp.broadcast_to(shifted[:, None, :], (walker_total, GROUP, held)).reshape(wide, held)
-        high, low = split_two(spread)
-        weights_ref[0:wide, :] = high
-        weights_ref[wide : 2 * wide, :] = low
-
-    source = lax.broadcasted_iota(jnp.int32, (held, block * GROUP), 0)
-    target = lax.broadcasted_iota(jnp.int32, (held, block * GROUP), 1)
-    chooser = (source == step * block + target // GROUP).astype(bf16)
-    mixed = dot_of(weights_ref[...], chooser)
-    rows = lax.broadcasted_iota(jnp.int32, mixed.shape, 0) % GROUP
-    cols = lax.broadcasted_iota(jnp.int32, mixed.shape, 1) % GROUP
-    mixed_ref[...] = jnp.where(rows == cols, mixed, 0.0).astype(bf16)
-    for group in range(slab_rows // GROUP):
-        chosen = vector_ref[:, group * GROUP : (group + 1) * GROUP, :]
-        both = dot_of(mixed_ref[...], chosen.reshape(block * GROUP, slab_cols))
-        added = both[:wide] + both[wide:]
-
-        @pl.when(step == 0)
-        def _():
-            total_ref[group] = added
-
-        @pl.when(step > 0)
-        def _():
-            total_ref[group] = total_ref[group] + added
-
-    @pl.when(step == pl.num_programs(0) - 1)
-    def _():
-        core = core_ref[0]
-        shape = (walker_total, GROUP, LANES)
-        for target_ref, place in ((keep_ref, core), (send_ref, 1 - core)):
-            for group in range(groups):
-                value = total_ref[place * groups + group]
-                target_ref[:, group * GROUP : (group + 1) * GROUP, :] = value[:, :LANES].reshape(shape)
-                if group < groups // 2:
-                    paired = total_ref[place * groups + group + groups // 2]
-                    tail = jnp.concatenate([value[:, LANES:], paired[:, LANES:]], axis=1)
-                    start = half + group * GROUP
-                    target_ref[:, start : start + GROUP, :] = tail.reshape(shape)
+        high, low = split_two(noise_ref[...] + root_step * bias)
+        weights_ref[...] = jnp.concatenate([high, low], axis=0)
+
+    for group in range(groups):
+        index = step * groups + group
+        both = dot_of(weights_ref[...], packed_rows(vector_ref, group), last_dims)
+        added = both[:walker_total] + both[walker_total:]
+        for row in range(GROUP):
+            out_ref[index * GROUP + row] = added[:, row * LANES : (row + 1) * LANES]
+        for row in range(GROUP // 2):
+            start = (GROUP + row) * LANES
+            out_ref[half + index * (GROUP // 2) + row] = added[:, start : start + LANES]
 
 
 def series_body(core_ref, own_ref, other_ref, walker_ref, out_ref, matrix_ref, *, row_groups, col_groups):
@@ -347,7 +311,8 @@
                 top = jnp.where(tail_lanes(even), even, half_rolled(odd))
                 bottom = jnp.where(tail_lanes(even), half_rolled(even), odd)
                 lane = (col_groups + col // 2) * LANES
-                joined = jnp.concatenate([top, bottom], axis=0).astype(bf16)
+                parts = [part.reshape(-1, 1, GROUP // 2, LANES) for part in (top, bottom)]
+                joined = jnp.concatenate(parts, axis=1).reshape(half, LANES).astype(bf16)
                 matrix_ref[pl.ds(start, half), lane : lane + LANES] = joined
 
     term = walker_ref[...]
@@ -368,16 +333,72 @@
 BLOCK = 32
 
 
+def bias_half(place, green, vectors, before, copies):
+    owners, dense, _ = green.shape
+    slab_rows, slab_cols, held = vectors.shape
+    steps = slab_rows // 2 // BLOCK
+    whole = lambda *shape: pl.BlockSpec(shape, lambda step, place: (0,) * len(shape))
+    return pl.pallas_call(
+        bias_body,
+        grid_spec=pltpu.PrefetchScalarGridSpec(
+            num_scalar_prefetch=1,
+            grid=(steps,),
+            in_specs=[
+                whole(owners, dense, LANES),
+                pl.BlockSpec(
+                    (BLOCK, slab_cols, held), lambda step, place: (place[0] * steps + step, 0, 0)
+                ),
+                whole(owners, held),
+            ],
+            out_specs=whole(copies, owners, held),
+            scratch_shapes=[
+                pltpu.VMEM((dense, owners, LANES), bf16),
+                pltpu.VMEM((owners, held), f32),
+            ],
+        ),
+        out_shape=jax.ShapeDtypeStruct((copies, owners, held), f32),
+        name="bias",
+    )(place, green, vectors, before)
+
+
+def potential_half(place, parts, noise, vectors):
+    count, owners, held = parts.shape
+    slab_rows, slab_cols, _ = vectors.shape
+    dense = slab_rows // 2 * 3 // 2
+    steps = slab_rows // 2 // BLOCK
+    whole = lambda *shape: pl.BlockSpec(shape, lambda step, place: (0,) * len(shape))
+    return pl.pallas_call(
+        potential_body,
+        grid_spec=pltpu.PrefetchScalarGridSpec(
+            num_scalar_prefetch=1,
+            grid=(steps,),
+            in_specs=[
+                whole(count, owners, held),
+                whole(owners, held),
+                pl.BlockSpec(
+                    (BLOCK, slab_cols, held), lambda step, place: (place[0] * steps + step, 0, 0)
+                ),
+            ],
+            out_specs=(whole(owners, held), whole(dense, owners, LANES)),
+            scratch_shapes=[pltpu.VMEM((2 * owners, held), bf16)],
+        ),
+        out_shape=(
+            jax.ShapeDtypeStruct((owners, held), f32),
+            jax.ShapeDtypeStruct((dense, owners, LANES), f32),
+        ),
+        name="potential",
+    )(place, parts, noise, vectors)
+
+
 def fast_shards(chol_vectors, trial_orbitals, walkers, field_noise):
     held, slab_rows, slab_cols = chol_vectors.shape
     orbital_count, electron_count = trial_orbitals.shape
     row_groups = lax.axis_size("pairs")
     col_groups = lax.axis_size("chol")
     owners = row_groups * col_groups
-    half = slab_rows // 2
-    dense = half + half // 2
-    wide = owners * GROUP
+    dense = slab_rows // 2 * 3 // 2
     core = lax.axis_index("walk").astype(jnp.int32).reshape(1)
+    vectors = jnp.transpose(chol_vectors, (1, 2, 0))
     own = walkers[0]
     other = swapped(own, "walk", 0)
     outgoing = pl.pallas_call(
@@ -391,38 +412,12 @@
     axes = ("pairs", "chol")
     arrived = lax.all_to_all(outgoing, axes, split_axis=0, concat_axis=0, tiled=True)
     arrived_other = swapped(arrived, "walk", 0)
-    blocks = pl.BlockSpec((BLOCK, slab_rows, slab_cols), lambda step: (step, 0, 0))
-    spread = pl.pallas_call(
-        functools.partial(bias_body, slab_rows=slab_rows, slab_cols=slab_cols),
-        grid=(held // BLOCK,),
-        out_shape=jax.ShapeDtypeStruct((owners, owners, held), f32),
-        in_specs=[smem, vmem, vmem, blocks],
-        out_specs=vmem,
-        scratch_shapes=[
-            pltpu.VMEM((slab_rows // GROUP, wide, slab_cols), bf16),
-            pltpu.VMEM((held, wide), f32),
-        ],
-        name="bias",
-    )(core, arrived, arrived_other, chol_vectors)
+    first = bias_half(core, arrived, vectors, jnp.zeros((owners, held), f32), 1)
+    spread = bias_half(1 - core, arrived_other, vectors, first[0], owners)
     parts = lax.all_to_all(spread, axes, split_axis=0, concat_axis=0, tiled=True)
-    force_bias, keep, send = pl.pallas_call(
-        functools.partial(potential_body, slab_rows=slab_rows, slab_cols=slab_cols),
-        grid=(held // BLOCK,),
-        out_shape=(
-            jax.ShapeDtypeStruct((owners, held), f32),
-            jax.ShapeDtypeStruct((owners, dense, LANES), f32),
-            jax.ShapeDtypeStruct((owners, dense, LANES), f32),
-        ),
-        in_specs=[smem, vmem, vmem, blocks],
-        out_specs=(vmem, vmem, vmem),
-        scratch_shapes=[
-            pltpu.VMEM((2 * wide, held), bf16),
-            pltpu.VMEM((2 * wide, BLOCK * GROUP), bf16),
-            pltpu.VMEM((slab_rows // GROUP, wide, slab_cols), f32),
-        ],
-        name="potential",
-    )(core, parts, field_noise[0], chol_vectors)
-    summed = (keep + swapped(send, "walk", 0)).astype(bf16)
+    force_bias, send = potential_half(1 - core, parts, field_noise[0], vectors)
+    _, keep = potential_half(core, parts, field_noise[0], vectors)
+    summed = jnp.swapaxes((keep + swapped(send, "walk", 0)).astype(bf16), 0, 1)
     received = lax.all_to_all(summed, axes, split_axis=0, concat_axis=0, tiled=True)
     received_other = swapped(received, "walk", 0)
     propagated = pl.pallas_call(
@@ -445,8 +440,7 @@
         and lax.axis_size("walk") == 2
         and lax.axis_size("chol") % 2 == 0
         and slab_cols == LANES + LANES // 2
-        and slab_rows % (4 * GROUP) == 0
-        and held % BLOCK == 0
+        and slab_rows % (2 * BLOCK) == 0
         and trial_orbitals.shape[1] % 256 == 0
         and field_noise.shape[0] == 1
     )

time: 187 us -> 116 us (0.62)
  Pallas kernels: 78.3 us -> 42 us
  local copies, waits for them, and re-layouts: 36.7 us -> 4.84 us
  waiting for transfers between devices: 6.62 us -> 3.57 us
    pallas_call x2 -> x4, Pallas kernels: 61.9 us -> 25.6 us  [the longest x2 13.7 us: potential_half(): pl.pallas_call(potential_body, grid_spec=pltpu.PrefetchScalarGridSpec(num...]
    unnamed x11 -> x10, local copies, waits for them, and re-layouts: 36.7 us -> 2.54 us
    ppermute x4, waiting for transfers between devices: 6.62 us -> 3.57 us  [swapped(): return lax.ppermute(value, axis, pairs)]
  transfers between devices with their start and end apart: 4 -> 4, of which waited for: 3 -> 2; matrix products, arithmetic and copies ran while one was open for 18% -> 1% of each run, Pallas kernels for 0% -> 11%
where the time goes in v1:
time: 116 us
  blocking collectives  62.2 us (54%)
  Pallas kernels  42 us (36%)
  local copies, waits for them, and re-layouts  4.84 us (4%)
  waiting for transfers between devices  3.57 us (3%)
  other arithmetic  1.67 us (1%)
    all_to_all x1, blocking collectives, fast_shards(): lax.all_to_all(outgoing, axes, split_axis=0, concat_axis=0, tiled=True)  26 us
    all_to_all x1, blocking collectives, fast_shards(): lax.all_to_all(summed, axes, split_axis=0, concat_axis=0, tiled=True)  21.4 us
    all_to_all x1, blocking collectives, fast_shards(): lax.all_to_all(spread, axes, split_axis=0, concat_axis=0, tiled=True)  14.8 us
    pallas_call x2, Pallas kernels, potential_half(): pl.pallas_call(potential_body, grid_spec=pltpu.PrefetchScalarGridSpec(num...  13.7 us
    pallas_call x2, Pallas kernels, bias_half(): pl.pallas_call(bias_body, grid_spec=pltpu.PrefetchScalarGridSpec(num_scal...  11.9 us
    pallas_call x1, Pallas kernels, fast_shards(): pl.pallas_call(functools.partial(green_body, row_groups=row_groups, col_g...  11.1 us
    pallas_call x1, Pallas kernels, fast_shards(): pl.pallas_call(functools.partial(series_body, row_groups=row_groups, col_...  5.27 us
    ppermute x4, waiting for transfers between devices, swapped(): return lax.ppermute(value, axis, pairs)  3.57 us
  transfers between devices with their start and end apart: 4, of which 2 were waited for; matrix products, arithmetic and copies ran while one was open for 1% of the time, Pallas kernels for 11%

profile of v1, /device:TPU:0, one launch (start us, length us, event | category | flops | bytes accessed | tf_op | source)
XLA Modules:
  0.0 115.5 jit_solution(7672161720070100411)
XLA Ops:
  0.6 0.6 collective-permute-start
  1.2 1.6 %collective-permute-done.other_ref = f32[768,128]{1,0:T(8,128)S(1)} collective-permute-done((f32[768,128]{1,0:T(8,128)}, f32[768,128]{1,0:T(8,128)S(1)}, u32[]{:S(2)}, u32[]{:S(2)}) %collective-permute-start) | collective-permute-done | bytes 393248 | tf_op jit(solution)/shard_map/ppermute | solution.py:24
  2.7 0.0 copy-start.4
  2.8 0.7 copy-done.4
  3.5 11.1 %green.1 = bf16[16,144,128]{2,1,0:T(8,128)(2,1)} custom-call(s32[1]{0:T(128)} %bitcast.core_ref.place_ref, f32[768,128]{1,0:T(8,128)} %bitcast.14, f32[768,128]{1,0:T(8,128)} %copy-done.4, f32[768,256]{1,0:T(8,128)} %trial_ref.1), custom_call_target="tpu_custom_call" | custom-call | tf_op jit(solution)/shard_map/green/pallas_call | solution.py:404
  14.6 26.0 %all_to_all.15.green_ref = bf16[16,144,128]{2,1,0:T(8,128)(2,1)S(1)} all-to-all(bf16[16,144,128]{2,1,0:T(8,128)(2,1)} %green.1), channel_id=1, replica_groups=mesh['groups'=1,'pairs'=4,'chol'=4,'walk'=2] {'pairs','chol'}, dimensions={0} | all-to-all | bytes 1179648 | tf_op jit(solution)/shard_map/all_to_all | solution.py:413
  40.6 0.0 copy-start
  40.6 0.0 collective-permute-start.1
  40.6 0.7 broadcast_in_dim.9.before_ref
  41.2 0.2 copy-done
  41.4 5.9 %bias.2 = f32[1,16,256]{2,1,0:T(8,128)} custom-call(s32[1]{0:T(128)} %bitcast.core_ref.place_ref, bf16[16,144,128]{2,1,0:T(8,128)(2,1)} %copy-done, bf16[192,192,256]{2,1,0:T(8,128)(2,1)} %bitcast.9, f32[16,256]{1,0:T(8,128)} %broadcast_in_dim.9.before_ref), custom_call_target="tpu_custom_call" | custom-call | tf_op jit(solution)/shard_map/bias/pallas_call | solution.py:341
  47.3 0.0 collective-permute-done.1.green_ref
  47.3 0.0 copy-start.2
  47.3 0.8 copy-done.2
  48.1 6.0 %bias.3 = f32[16,16,256]{2,1,0:T(8,128)} custom-call(s32[1]{0:T(128)S(6)} %sub.4.place_ref, bf16[16,144,128]{2,1,0:T(8,128)(2,1)} %copy-done.2, bf16[192,192,256]{2,1,0:T(8,128)(2,1)} %bitcast.10, f32[16,256]{1,0:T(8,128)} %bitcast.19), custom_call_target="tpu_custom_call" | custom-call | tf_op jit(solution)/shard_map/bias/pallas_call | solution.py:341
  54.1 14.8 %all_to_all.16.parts_ref = f32[16,16,256]{2,1,0:T(8,128)} all-to-all(f32[16,16,256]{2,1,0:T(8,128)} %bias.3), channel_id=1, replica_groups=mesh['groups'=1,'pairs'=4,'chol'=4,'walk'=2] {'pairs','chol'}, dimensions={0} | all-to-all | bytes 524288 | tf_op jit(solution)/shard_map/all_to_all | solution.py:417
  68.8 6.9 %potential.3 = (f32[16,256]{1,0:T(8,128)}, f32[144,16,128]{2,1,0:T(8,128)}) custom-call(s32[1]{0:T(128)S(6)} %sub.4.place_ref, f32[16,16,256]{2,1,0:T(8,128)} %all_to_all.16.parts_ref, f32[16,256]{1,0:T(8,128)} %bitcast.17, bf16[192,192,256]{2,1,0:T(8,128)(2,1)} %bitcast.11), custom_call_target="tpu_custom_call" | custom-call | tf_op jit(solution)/shard_map/potential/pallas_call | solution.py:370
  75.7 1.7 %copy.6 = f32[144,16,128]{2,0,1:T(8,128)S(1)} copy(f32[144,16,128]{2,1,0:T(8,128)} %get-tuple-element.6) | data formatting | bytes 2359296 | tf_op jit(solution)/shard_map/potential/pallas_call | solution.py:370
  77.4 0.1 collective-permute-start.2
  77.4 6.9 %potential.2 = (f32[16,256]{1,0:T(8,128)}, f32[144,16,128]{2,1,0:T(8,128)}) custom-call(s32[1]{0:T(128)} %bitcast.core_ref.place_ref, f32[16,16,256]{2,1,0:T(8,128)} %all_to_all.16.parts_ref, f32[16,256]{1,0:T(8,128)} %bitcast.18, bf16[192,192,256]{2,1,0:T(8,128)(2,1)} %bitcast.12), custom_call_target="tpu_custom_call" | custom-call | tf_op jit(solution)/shard_map/potential/pallas_call | solution.py:370
  84.3 0.0 collective-permute-done.2
  84.3 1.7 %fusion.1 = bf16[16,144,128]{2,1,0:T(8,128)(2,1)S(1)} fusion(f32[144,16,128]{2,0,1:T(8,128)S(1)} %collective-permute-done.2, f32[144,16,128]{2,1,0:T(8,128)} %get-tuple-element.5), kind=kLoop, calls=%fused_computation.2 | loop fusion | flops 589824 | bytes 2949120 | tf_op jit(solution)/shard_map/transpose | solution.py:420
  86.0 21.4 %all_to_all.17.own_ref = bf16[16,144,128]{2,1,0:T(8,128)(2,1)S(1)} all-to-all(bf16[16,144,128]{2,1,0:T(8,128)(2,1)S(1)} %fusion.1), channel_id=1, replica_groups=mesh['groups'=1,'pairs'=4,'chol'=4,'walk'=2] {'pairs','chol'}, dimensions={0} | all-to-all | bytes 1179648 | tf_op jit(solution)/shard_map/all_to_all | solution.py:421
  107.4 0.0 copy-start.1
  107.4 0.0 collective-permute-start.3
  107.4 2.0 %collective-permute-done.3.other_ref = bf16[16,144,128]{2,1,0:T(8,128)(2,1)S(1)} collective-permute-done((bf16[16,144,128]{2,1,0:T(8,128)(2,1)S(1)}, bf16[16,144,128]{2,1,0:T(8,128)(2,1)S(1)}, u32[]{:S(2)}, u32[]{:S(2)}) %collective-permute-start.3) | collective-permute-done | bytes 589856 | tf_op jit(solution)/shard_map/ppermute | solution.py:24
  109.4 0.0 copy-done.1
  109.4 0.0 copy-start.3
  109.4 0.8 copy-done.3
  110.2 5.3 %series.1 = f32[768,128]{1,0:T(8,128)} custom-call(s32[1]{0:T(128)} %bitcast.core_ref.place_ref, bf16[16,144,128]{2,1,0:T(8,128)(2,1)} %copy-done.1, bf16[16,144,128]{2,1,0:T(8,128)(2,1)} %copy-done.3, f32[768,128]{1,0:T(8,128)} %bitcast.15), custom_call_target="tpu_custom_call" | custom-call | tf_op jit(solution)/shard_map/series/pallas_call | solution.py:423
Async XLA Ops:
  0.6 2.1 %collective-permute-start = (f32[768,128]{1,0:T(8,128)}, f32[768,128]{1,0:T(8,128)S(1)}, u32[]{:S(2)}, u32[]{:S(2)}) collective-permute-start(f32[768,128]{1,0:T(8,128)} %bitcast.13), channel_id=1, source_target_pairs={{0,1},{1,0},{2,3},{3,2},{4,5},{5,4},{6,7},{7,6},{8,9},{9,8},{10,11... | collective-permute-start | bytes 1179656 | tf_op jit(solution)/shard_map/ppermute | solution.py:24
  2.7 0.7 copy-start.4
  40.6 0.8 copy-start
  40.6 6.7 %collective-permute-start.1 = (bf16[16,144,128]{2,1,0:T(8,128)(2,1)S(1)}, bf16[16,144,128]{2,1,0:T(8,128)(2,1)S(1)}, u32[]{:S(2)}, u32[]{:S(2)}) collective-permute-start(bf16[16,144,128]{2,1,0:T(8,128)(2,1)S(1)} %all_to_all.15.green_ref), channel_id=1, source_target_pairs={{0,1},{1,0},{2,3},{3,2},{4,5},{5,4},{6,7},{7,6},{8,9},{9,8},{10,11... | collective-permute-start | bytes 1769480 | tf_op jit(solution)/shard_map/ppermute | solution.py:24
  47.3 0.8 copy-start.2
  77.4 7.0 %collective-permute-start.2 = (f32[144,16,128]{2,0,1:T(8,128)S(1)}, f32[144,16,128]{2,0,1:T(8,128)S(1)}, u32[]{:S(2)}, u32[]{:S(2)}) collective-permute-start(f32[144,16,128]{2,0,1:T(8,128)S(1)} %copy.6), channel_id=1, source_target_pairs={{0,1},{1,0},{2,3},{3,2},{4,5},{5,4},{6,7},{7,6},{8,9},{9,8},{10,11... | collective-permute-start | bytes 3538952 | tf_op jit(solution)/shard_map/ppermute | solution.py:24
  107.4 2.0 %copy-start.1 = (bf16[16,144,128]{2,1,0:T(8,128)(2,1)}, bf16[16,144,128]{2,1,0:T(8,128)(2,1)S(1)}, u32[]{:S(2)}) copy-start(bf16[16,144,128]{2,1,0:T(8,128)(2,1)S(1)} %all_to_all.17.own_ref) | copy-start | bytes 1769476
  107.4 2.0 %collective-permute-start.3 = (bf16[16,144,128]{2,1,0:T(8,128)(2,1)S(1)}, bf16[16,144,128]{2,1,0:T(8,128)(2,1)S(1)}, u32[]{:S(2)}, u32[]{:S(2)}) collective-permute-start(bf16[16,144,128]{2,1,0:T(8,128)(2,1)S(1)} %all_to_all.17.own_ref), channel_id=1, source_target_pairs={{0,1},{1,0},{2,3},{3,2},{4,5},{5,4},{6,7},{7,6},{8,9},{9,8},{10,11... | collective-permute-start | bytes 1769480 | tf_op jit(solution)/shard_map/ppermute | solution.py:24
  109.4 0.8 copy-start.3

commit v2 on v1

--- a/solution.py
+++ b/solution.py
@@ -12,8 +12,9 @@
 
 root_step = 0.05
 highest = lax.Precision.HIGHEST
-GROUP = 16
 LANES = 128
+SUB = LANES // 2
+SUBS = 3
 f32 = jnp.float32
 bf16 = jnp.bfloat16
 
@@ -163,12 +164,11 @@
     return found
 
 
-def green_body(core_ref, own_ref, other_ref, trial_ref, out_ref, inverse_ref, matrix_ref, *, row_groups, col_groups):
+def green_body(core_ref, own_ref, other_ref, trial_ref, out_ref, inverse_ref, matrix_ref, solved_ref, *, row_groups, col_groups):
     orbital_count, electron_count = trial_ref.shape
     slab_rows = orbital_count // row_groups
     slab_cols = orbital_count // col_groups
     core = core_ref[0]
-    half = slab_rows // 2
     walker = jnp.concatenate([own_ref[...], other_ref[...]], axis=1)
     trial = trial_ref[...]
     inter = dot_of(trial, walker, first_dims, highest)
@@ -204,60 +204,52 @@
         refine,
         (jnp.int32(0), jnp.float32(1e30)),
     )
-    chosen = []
-    for row in range(row_groups):
-        start = pl.multiple_of(row * slab_rows + core * half, 8)
-        chosen.append(
-            jnp.concatenate(
-                [own_ref[pl.ds(start, half), :], other_ref[pl.ds(start, half), :]], axis=1
-            )
-        )
-    scaled = dot_three(jnp.concatenate(chosen, axis=0), inverse_ref[...]) * inverse_scale
-    pieces = [trial_ref[slab_cols * c : slab_cols * c + LANES, :] for c in range(col_groups)]
-    pieces += [trial_ref[slab_cols * c + LANES : slab_cols * (c + 1), :] for c in range(col_groups)]
-    green = dot_three(scaled, jnp.concatenate(pieces, axis=0), last_dims)
-    quarter = half // 2
-    for row in range(row_groups):
+    walker_rows = dot_three(
+        jnp.concatenate([own_ref[...], other_ref[...]], axis=1), inverse_ref[...]
+    )
+    solved_ref[...] = walker_rows * inverse_scale
+    part = SUB // 2
+    empty = jnp.zeros((SUB, electron_count), f32)
+    for sub in range(SUBS):
+        following = (sub + 1) % SUBS
+        starts = [
+            pl.multiple_of(row * slab_rows + sub * SUB + core * part, 8) for row in range(row_groups)
+        ]
+        left = jnp.concatenate([solved_ref[pl.ds(start, part), :] for start in starts], axis=0)
+        left_turned = jnp.concatenate([trial_ref[pl.ds(start, part), :] for start in starts], axis=0)
+        right = []
+        right_turned = []
         for col in range(col_groups):
-            place = row * col_groups + col
-            slab = green[row * half : (row + 1) * half]
-            out_ref[place, 0:half, :] = slab[:, col * LANES : (col + 1) * LANES].astype(bf16)
-            start = (col_groups + col // 2) * LANES
-            tails = slab[:, start : start + LANES].reshape(-1, 2, GROUP // 2, LANES)
-            top = tails[:, 0].reshape(quarter, LANES)
-            bottom = tails[:, 1].reshape(quarter, LANES)
-            if col % 2 == 0:
-                packed = jnp.where(tail_lanes(top), top, half_rolled(bottom))
-            else:
-                packed = jnp.where(tail_lanes(top), half_rolled(top), bottom)
-            out_ref[place, half : half + quarter, :] = packed.astype(bf16)
-
-
-def packed_rows(vector_ref, group):
-    chosen = vector_ref[group * GROUP : (group + 1) * GROUP]
-    pieces = [chosen[row, :LANES] for row in range(GROUP)]
-    for row in range(GROUP // 2):
-        pieces += [chosen[row, LANES:], chosen[row + GROUP // 2, LANES:]]
-    return jnp.concatenate(pieces, axis=0)
-
-
-def bias_body(place_ref, green_ref, vector_ref, before_ref, out_ref, turned_ref, total_ref):
+            same = col * slab_cols + sub * SUB
+            next_one = col * slab_cols + following * SUB
+            right += [trial_ref[same : same + SUB, :], trial_ref[next_one : next_one + SUB, :]]
+            right_turned += [empty, solved_ref[next_one : next_one + SUB, :]]
+        green = dot_three(left, jnp.concatenate(right, axis=0), last_dims)
+        turned = dot_three(left_turned, jnp.concatenate(right_turned, axis=0), last_dims)
+        summed = green.astype(bf16).astype(f32) + turned.astype(bf16).astype(f32)
+        summed = summed.astype(bf16)
+        for row in range(row_groups):
+            for col in range(col_groups):
+                out_ref[row * col_groups + col, sub * part : (sub + 1) * part, :] = summed[
+                    row * part : (row + 1) * part, col * LANES : (col + 1) * LANES
+                ]
+
+
+def bias_body(place_ref, green_ref, same_ref, next_ref, before_ref, out_ref, turned_ref, total_ref):
     step = pl.program_id(0)
-    groups = vector_ref.shape[0] // GROUP
-    half = pl.num_programs(0) * groups * GROUP
+    block = same_ref.shape[0]
 
     @pl.when(step == 0)
     def _():
         turned_ref[...] = jnp.swapaxes(green_ref[...].astype(f32), 0, 1).astype(bf16)
         total_ref[...] = before_ref[...]
 
-    total = total_ref[...]
-    for group in range(groups):
-        index = step * groups + group
-        pieces = [turned_ref[index * GROUP + row] for row in range(GROUP)]
-        pieces += [turned_ref[half + index * (GROUP // 2) + row] for row in range(GROUP // 2)]
-        total = total + dot_of(jnp.concatenate(pieces, axis=1), packed_rows(vector_ref, group))
-    total_ref[...] = total
+    left = [turned_ref[step * block + row] for row in range(block)]
+    right = []
+    for row in range(block):
+        right += [same_ref[row], next_ref[row]]
+    total = dot_of(jnp.concatenate(left, axis=1), jnp.concatenate(right, axis=0))
+    total_ref[...] = total_ref[...] + total
 
     @pl.when(step == pl.num_programs(0) - 1)
     def _():
@@ -265,11 +257,10 @@
             out_ref[device] = total_ref[...]
 
 
-def potential_body(place_ref, parts_ref, noise_ref, vector_ref, bias_ref, out_ref, weights_ref):
+def potential_body(place_ref, parts_ref, noise_ref, same_ref, next_ref, bias_ref, out_ref, weights_ref):
     step = pl.program_id(0)
     walker_total = noise_ref.shape[0]
-    groups = vector_ref.shape[0] // GROUP
-    half = pl.num_programs(0) * groups * GROUP
+    block = same_ref.shape[0]
 
     @pl.when(step == 0)
     def _():
@@ -280,74 +271,88 @@
         high, low = split_two(noise_ref[...] + root_step * bias)
         weights_ref[...] = jnp.concatenate([high, low], axis=0)
 
-    for group in range(groups):
-        index = step * groups + group
-        both = dot_of(weights_ref[...], packed_rows(vector_ref, group), last_dims)
-        added = both[:walker_total] + both[walker_total:]
-        for row in range(GROUP):
-            out_ref[index * GROUP + row] = added[:, row * LANES : (row + 1) * LANES]
-        for row in range(GROUP // 2):
-            start = (GROUP + row) * LANES
-            out_ref[half + index * (GROUP // 2) + row] = added[:, start : start + LANES]
+    right = []
+    for row in range(block):
+        right += [same_ref[row], next_ref[row]]
+    both = dot_of(weights_ref[...], jnp.concatenate(right, axis=0), last_dims)
+    added = both[:walker_total] + both[walker_total:]
+    for row in range(block):
+        out_ref[step * block + row] = added[:, row * LANES : (row + 1) * LANES]
 
 
 def series_body(core_ref, own_ref, other_ref, walker_ref, out_ref, matrix_ref, *, row_groups, col_groups):
-    orbital_count = walker_ref.shape[0]
-    slab_rows = orbital_count // row_groups
-    slab_cols = orbital_count // col_groups
-    half = slab_rows // 2
-    quarter = half // 2
+    slab = SUB * SUBS
+    part = SUB // 2
+    size = row_groups * SUB
     core = core_ref[0]
     for source, place in ((own_ref, core), (other_ref, 1 - core)):
+        for sub in range(SUBS):
+            following = (sub + 1) % SUBS
+            for row in range(row_groups):
+                start = pl.multiple_of(sub * size + row * SUB + place * part, 16)
+                for col in range(0, col_groups, 2):
+                    index = row * col_groups + col
+                    even = source[index, sub * part : (sub + 1) * part, :].astype(f32)
+                    odd = source[index + 1, sub * part : (sub + 1) * part, :].astype(f32)
+                    same = jnp.where(tail_lanes(even), even, half_rolled(odd)).astype(bf16)
+                    beside = jnp.where(tail_lanes(even), half_rolled(even), odd).astype(bf16)
+                    lane = col // 2 * LANES
+                    matrix_ref[pl.ds(start, part), sub * size + lane : sub * size + lane + LANES] = same
+                    lane += following * size
+                    matrix_ref[pl.ds(start, part), lane : lane + LANES] = beside
+    for sub in range(SUBS):
+        following = (sub + 1) % SUBS
+        block = matrix_ref[sub * size : (sub + 1) * size, following * size : (following + 1) * size]
+        matrix_ref[following * size : (following + 1) * size, sub * size : (sub + 1) * size] = (
+            block.astype(f32).T.astype(bf16)
+        )
+
+    pieces = []
+    for sub in range(SUBS):
         for row in range(row_groups):
-            start = pl.multiple_of(row * slab_rows + place * half, GROUP)
-            for col in range(col_groups):
-                index = row * col_groups + col
-                matrix_ref[pl.ds(start, half), col * LANES : (col + 1) * LANES] = source[index, 0:half, :]
-            for col in range(0, col_groups, 2):
-                index = row * col_groups + col
-                even = source[index, half : half + quarter, :].astype(f32)
-                odd = source[index + 1, half : half + quarter, :].astype(f32)
-                top = jnp.where(tail_lanes(even), even, half_rolled(odd))
-                bottom = jnp.where(tail_lanes(even), half_rolled(even), odd)
-                lane = (col_groups + col // 2) * LANES
-                parts = [part.reshape(-1, 1, GROUP // 2, LANES) for part in (top, bottom)]
-                joined = jnp.concatenate(parts, axis=1).reshape(half, LANES).astype(bf16)
-                matrix_ref[pl.ds(start, half), lane : lane + LANES] = joined
-
-    term = walker_ref[...]
+            pieces.append(walker_ref[row * slab + sub * SUB : row * slab + (sub + 1) * SUB, :])
+    term = jnp.concatenate(pieces, axis=0)
     total = term
     width = term.shape[1]
     for degree in range(1, TERMS):
-        order = [term[slab_cols * c : slab_cols * c + LANES] for c in range(col_groups)]
-        order += [term[slab_cols * c + LANES : slab_cols * (c + 1)] for c in range(col_groups)]
-        high, low = split_two(jnp.concatenate(order, axis=0))
+        high, low = split_two(term)
         both = dot_of(matrix_ref[...], jnp.concatenate([high, low], axis=1))
         term = (-root_step / degree) * (both[:, :width] + both[:, width:])
         total = total + term
-    out_ref[...] = total
+    for sub in range(SUBS):
+        for row in range(row_groups):
+            start = sub * size + row * SUB
+            out_ref[row * slab + sub * SUB : row * slab + (sub + 1) * SUB, :] = total[start : start + SUB]
 
 
 smem = pl.BlockSpec(memory_space=pltpu.SMEM)
 vmem = pl.BlockSpec(memory_space=pltpu.VMEM)
-BLOCK = 32
+grant = pltpu.CompilerParams(vmem_limit_bytes=16 * 2**20)
+large_grant = pltpu.CompilerParams(vmem_limit_bytes=46 * 2**20)
+
+
+def whole(*shape):
+    return pl.BlockSpec(shape, lambda step, place: (0,) * len(shape))
+
+
+def half_blocks(held, shift):
+    return pl.BlockSpec(
+        (SUB // 2, SUB, held), lambda step, place: (2 * step + place[0], (step + shift) % SUBS, 0)
+    )
 
 
 def bias_half(place, green, vectors, before, copies):
     owners, dense, _ = green.shape
-    slab_rows, slab_cols, held = vectors.shape
-    steps = slab_rows // 2 // BLOCK
-    whole = lambda *shape: pl.BlockSpec(shape, lambda step, place: (0,) * len(shape))
+    held = vectors.shape[2]
     return pl.pallas_call(
         bias_body,
         grid_spec=pltpu.PrefetchScalarGridSpec(
             num_scalar_prefetch=1,
-            grid=(steps,),
+            grid=(SUBS,),
             in_specs=[
                 whole(owners, dense, LANES),
-                pl.BlockSpec(
-                    (BLOCK, slab_cols, held), lambda step, place: (place[0] * steps + step, 0, 0)
-                ),
+                half_blocks(held, 0),
+                half_blocks(held, 1),
                 whole(owners, held),
             ],
             out_specs=whole(copies, owners, held),
@@ -357,27 +362,24 @@
             ],
         ),
         out_shape=jax.ShapeDtypeStruct((copies, owners, held), f32),
+        compiler_params=large_grant,
         name="bias",
-    )(place, green, vectors, before)
+    )(place, green, vectors, vectors, before)
 
 
 def potential_half(place, parts, noise, vectors):
     count, owners, held = parts.shape
-    slab_rows, slab_cols, _ = vectors.shape
-    dense = slab_rows // 2 * 3 // 2
-    steps = slab_rows // 2 // BLOCK
-    whole = lambda *shape: pl.BlockSpec(shape, lambda step, place: (0,) * len(shape))
+    dense = SUBS * SUB // 2
     return pl.pallas_call(
         potential_body,
         grid_spec=pltpu.PrefetchScalarGridSpec(
             num_scalar_prefetch=1,
-            grid=(steps,),
+            grid=(SUBS,),
             in_specs=[
                 whole(count, owners, held),
                 whole(owners, held),
-                pl.BlockSpec(
-                    (BLOCK, slab_cols, held), lambda step, place: (place[0] * steps + step, 0, 0)
-                ),
+                half_blocks(held, 0),
+                half_blocks(held, 1),
             ],
             out_specs=(whole(owners, held), whole(dense, owners, LANES)),
             scratch_shapes=[pltpu.VMEM((2 * owners, held), bf16)],
@@ -386,27 +388,30 @@
             jax.ShapeDtypeStruct((owners, held), f32),
             jax.ShapeDtypeStruct((dense, owners, LANES), f32),
         ),
+        compiler_params=large_grant,
         name="potential",
-    )(place, parts, noise, vectors)
+    )(place, parts, noise, vectors, vectors)
 
 
 def fast_shards(chol_vectors, trial_orbitals, walkers, field_noise):
-    held, slab_rows, slab_cols = chol_vectors.shape
+    held = chol_vectors.shape[0]
     orbital_count, electron_count = trial_orbitals.shape
     row_groups = lax.axis_size("pairs")
     col_groups = lax.axis_size("chol")
     owners = row_groups * col_groups
-    dense = slab_rows // 2 * 3 // 2
+    dense = SUBS * SUB // 2
     core = lax.axis_index("walk").astype(jnp.int32).reshape(1)
     vectors = jnp.transpose(chol_vectors, (1, 2, 0))
     own = walkers[0]
     other = swapped(own, "walk", 0)
+    square = pltpu.VMEM((electron_count, electron_count), f32)
     outgoing = pl.pallas_call(
         functools.partial(green_body, row_groups=row_groups, col_groups=col_groups),
         out_shape=jax.ShapeDtypeStruct((owners, dense, LANES), bf16),
         in_specs=[smem, vmem, vmem, vmem],
         out_specs=vmem,
-        scratch_shapes=[pltpu.VMEM((electron_count, electron_count), f32)] * 2,
+        scratch_shapes=[square, square, pltpu.VMEM((orbital_count, electron_count), f32)],
+        compiler_params=grant,
         name="green",
     )(core, own, other, trial_orbitals)
     axes = ("pairs", "chol")
@@ -426,6 +431,7 @@
         in_specs=[smem, vmem, vmem, vmem],
         out_specs=vmem,
         scratch_shapes=[pltpu.VMEM((orbital_count, orbital_count), bf16)],
+        compiler_params=grant,
         name="series",
     )(core, received, received_other, own)
     return propagated[None], force_bias[None]
@@ -433,15 +439,15 @@
 
 def packable(chol_vectors, trial_orbitals, walkers, field_noise):
     held, slab_rows, slab_cols = chol_vectors.shape
-    owners = lax.axis_size("pairs") * lax.axis_size("chol")
+    row_groups = lax.axis_size("pairs")
     return (
         walkers.shape[0] == 1
-        and owners * GROUP <= 512
         and lax.axis_size("walk") == 2
-        and lax.axis_size("chol") % 2 == 0
-        and slab_cols == LANES + LANES // 2
-        and slab_rows % (2 * BLOCK) == 0
-        and trial_orbitals.shape[1] % 256 == 0
+        and lax.axis_size("chol") == row_groups
+        and row_groups in (2, 4, 8)
+        and slab_cols == slab_rows == SUB * SUBS
+        and held % LANES == 0
+        and trial_orbitals.shape[1] % LANES == 0
         and field_noise.shape[0] == 1
     )
 

time: 116 us -> 91.7 us (0.79)
  blocking collectives: 62.2 us -> 51.4 us
  Pallas kernels: 42 us -> 32.5 us
  local copies, waits for them, and re-layouts: 4.84 us -> 2.4 us
  other arithmetic: 1.67 us -> 0.27 us
    all_to_all x1, blocking collectives: 26 us -> 20.9 us  [fast_shards(): lax.all_to_all(outgoing, axes, split_axis=0, concat_axis=0, tiled=True)]
    all_to_all x1, blocking collectives: 21.4 us -> 16.6 us  [fast_shards(): lax.all_to_all(summed, axes, split_axis=0, concat_axis=0, tiled=True)]
    pallas_call x2, Pallas kernels: 13.7 us -> 9.96 us  [potential_half(): pl.pallas_call(potential_body, grid_spec=pltpu.PrefetchScalarGridSpec(num...]
    pallas_call x2, Pallas kernels: 11.9 us -> 8.25 us  [bias_half(): pl.pallas_call(bias_body, grid_spec=pltpu.PrefetchScalarGridSpec(num_scal...]
    transpose x1, other arithmetic: 1.67 us -> 0.27 us  [fast_shards(): summed = jnp.swapaxes((keep + swapped(send, 'walk', 0)).astype(bf16), 0, 1)]
    pallas_call x1, local copies, waits for them, and re-layouts: 1.65 us -> 0.25 us  [potential_half(): pl.pallas_call(potential_body, grid_spec=pltpu.PrefetchScalarGridSpec(num...]
    pallas_call x1, Pallas kernels: 5.27 us -> 3.96 us  [fast_shards(): pl.pallas_call(functools.partial(series_body, row_groups=row_groups, col_...]
    unnamed x10 -> x8, local copies, waits for them, and re-layouts: 2.54 us -> 2.14 us
  transfers between devices with their start and end apart: 4 -> 4, of which waited for: 2 -> 2; matrix products, arithmetic and copies ran while one was open for 1% -> 0% of each run, Pallas kernels for 11% -> 10%
where the time goes in v2:
time: 91.7 us; the launch traced here: 91.2 us
  blocking collectives  51.4 us (56%)
  Pallas kernels  32.5 us (35%)
  waiting for transfers between devices  3.29 us (4%)
  local copies, waits for them, and re-layouts  2.4 us (3%)
    all_to_all x1, blocking collectives, fast_shards(): lax.all_to_all(outgoing, axes, split_axis=0, concat_axis=0, tiled=True)  20.9 us
    all_to_all x1, blocking collectives, fast_shards(): lax.all_to_all(summed, axes, split_axis=0, concat_axis=0, tiled=True)  16.6 us
    all_to_all x1, blocking collectives, fast_shards(): lax.all_to_all(spread, axes, split_axis=0, concat_axis=0, tiled=True)  13.9 us
    pallas_call x1, Pallas kernels, fast_shards(): pl.pallas_call(functools.partial(green_body, row_groups=row_groups, col_g...  10.4 us
    pallas_call x2, Pallas kernels, potential_half(): pl.pallas_call(potential_body, grid_spec=pltpu.PrefetchScalarGridSpec(num...  9.96 us
    pallas_call x2, Pallas kernels, bias_half(): pl.pallas_call(bias_body, grid_spec=pltpu.PrefetchScalarGridSpec(num_scal...  8.25 us
    pallas_call x1, Pallas kernels, fast_shards(): pl.pallas_call(functools.partial(series_body, row_groups=row_groups, col_...  3.96 us
    ppermute x4, waiting for transfers between devices, swapped(): return lax.ppermute(value, axis, pairs)  3.29 us
  transfers between devices with their start and end apart: 4, of which 2 were waited for; matrix products, arithmetic and copies ran while one was open for 0% of the time, Pallas kernels for 10%

profile of v2, /device:TPU:0, one launch (start us, length us, event | category | flops | bytes accessed | tf_op | source)
XLA Modules:
  0.0 91.2 jit_solution(14181952934046403199)
XLA Ops:
  0.6 0.6 collective-permute-start
  1.2 1.6 %collective-permute-done.other_ref = f32[768,128]{1,0:T(8,128)S(1)} collective-permute-done((f32[768,128]{1,0:T(8,128)}, f32[768,128]{1,0:T(8,128)S(1)}, u32[]{:S(2)}, u32[]{:S(2)}) %collective-permute-start) | collective-permute-done | bytes 393248 | tf_op jit(solution)/shard_map/ppermute | solution.py:25
  2.7 0.0 copy-start
  2.8 1.0 %copy-done = f32[1,768,128]{2,1,0:T(8,128)S(1)} copy-done((f32[1,768,128]{2,1,0:T(8,128)S(1)}, f32[1,768,128]{2,1,0:T(8,128)}, u32[]{:S(2)}) %copy-start) | copy-done | bytes 393240
  3.7 0.0 copy-start.2
  3.7 1.1 %copy-done.2 = f32[768,256]{1,0:T(8,128)S(1)} copy-done((f32[768,256]{1,0:T(8,128)S(1)}, f32[768,256]{1,0:T(8,128)}, u32[]{:S(2)}) %copy-start.2) | copy-done | bytes 786456
  4.9 10.4 %green.1 = bf16[16,96,128]{2,1,0:T(8,128)(2,1)S(1)} custom-call(s32[1]{0:T(128)} %bitcast.core_ref.place_ref, f32[768,128]{1,0:T(8,128)S(1)} %bitcast.10, f32[768,128]{1,0:T(8,128)S(1)} %collective-permute-done.other_ref, f32[768,256]{1,0:T(8,128)S(1)} %copy-done.2), custom_call_target="tpu_custom_call" | custom-call | tf_op jit(solution)/shard_map/green/pallas_call | solution.py:408
  15.2 20.9 %all_to_all.15.green_ref = bf16[16,96,128]{2,1,0:T(8,128)(2,1)S(1)} all-to-all(bf16[16,96,128]{2,1,0:T(8,128)(2,1)S(1)} %green.1), channel_id=1, replica_groups=mesh['groups'=1,'pairs'=4,'chol'=4,'walk'=2] {'pairs','chol'}, dimensions={0} | all-to-all | bytes 786432 | tf_op jit(solution)/shard_map/all_to_all | solution.py:418
  36.2 0.0 collective-permute-start.1
  36.2 4.1 %bias.2 = f32[1,16,256]{2,1,0:T(8,128)S(1)} custom-call(s32[1]{0:T(128)} %bitcast.core_ref.place_ref, bf16[16,96,128]{2,1,0:T(8,128)(2,1)S(1)} %all_to_all.15.green_ref, bf16[192,192,256]{2,1,0:T(8,128)(2,1)} %bitcast.15, bf16[192,192,256]{2,1,0:T(8,128)(2,1)} %bitcast.16, f32[16,256]{1,0:T(8,128)S(1)} %broadcast_in_dim.9.before_ref), custom_call_target="tpu_custom_call" | custom-call | tf_op jit(solution)/shard_map/bias/pallas_call | solution.py:347
  40.3 0.0 collective-permute-done.1.green_ref
  40.3 0.0 copy-start.3
  40.3 4.2 %bias.3 = f32[16,16,256]{2,1,0:T(8,128)S(1)} custom-call(s32[1]{0:T(128)S(6)} %sub.4.place_ref, bf16[16,96,128]{2,1,0:T(8,128)(2,1)S(1)} %collective-permute-done.1.green_ref, bf16[192,192,256]{2,1,0:T(8,128)(2,1)} %bitcast.17, bf16[192,192,256]{2,1,0:T(8,128)(2,1)} %bitcast.18, f32[16,256]{1,0:T(8,128)S(1)} %bitcast.14), custom_call_target="tpu_custom_call" | custom-call | tf_op jit(solution)/shard_map/bias/pallas_call | solution.py:347
  44.5 13.9 %all_to_all.16.parts_ref = f32[16,16,256]{2,1,0:T(8,128)S(1)} all-to-all(f32[16,16,256]{2,1,0:T(8,128)S(1)} %bias.3), channel_id=1, replica_groups=mesh['groups'=1,'pairs'=4,'chol'=4,'walk'=2] {'pairs','chol'}, dimensions={0} | all-to-all | bytes 524288 | tf_op jit(solution)/shard_map/all_to_all | solution.py:422
  58.4 0.0 copy-done.3
  58.4 5.0 %potential.3 = (f32[16,256]{1,0:T(8,128)}, f32[96,16,128]{2,1,0:T(8,128)S(1)}) custom-call(s32[1]{0:T(128)S(6)} %sub.4.place_ref, f32[16,16,256]{2,1,0:T(8,128)S(1)} %all_to_all.16.parts_ref, f32[16,256]{1,0:T(8,128)S(1)} %bitcast.12, bf16[192,192,256]{2,1,0:T(8,128)(2,1)} %bitcast.19, bf16[192,192,256]{2,1,0:T(8,128)(2,1)} %bitcast.20), custom_call_target="tpu_custom_call" | custom-call | tf_op jit(solution)/shard_map/potential/pallas_call | solution.py:373
  63.4 0.3 copy.6
  63.6 0.0 copy-start.1
  63.6 0.1 collective-permute-start.2
  63.7 5.0 %potential.2 = (f32[16,256]{1,0:T(8,128)}, f32[96,16,128]{2,1,0:T(8,128)S(1)}) custom-call(s32[1]{0:T(128)} %bitcast.core_ref.place_ref, f32[16,16,256]{2,1,0:T(8,128)S(1)} %all_to_all.16.parts_ref, f32[16,256]{1,0:T(8,128)S(1)} %bitcast.13, bf16[192,192,256]{2,1,0:T(8,128)(2,1)} %bitcast.21, bf16[192,192,256]{2,1,0:T(8,128)(2,1)} %bitcast.22), custom_call_target="tpu_custom_call" | custom-call | tf_op jit(solution)/shard_map/potential/pallas_call | solution.py:373
  68.7 0.0 collective-permute-done.2
  68.7 0.3 fusion.1
  69.0 16.6 %all_to_all.17.own_ref = bf16[16,96,128]{2,1,0:T(8,128)(2,1)S(1)} all-to-all(bf16[16,96,128]{2,1,0:T(8,128)(2,1)S(1)} %fusion.1), channel_id=1, replica_groups=mesh['groups'=1,'pairs'=4,'chol'=4,'walk'=2] {'pairs','chol'}, dimensions={0} | all-to-all | bytes 786432 | tf_op jit(solution)/shard_map/all_to_all | solution.py:426
  85.5 0.0 collective-permute-start.3
  85.5 1.7 %collective-permute-done.3.other_ref = bf16[16,96,128]{2,1,0:T(8,128)(2,1)S(1)} collective-permute-done((bf16[16,96,128]{2,1,0:T(8,128)(2,1)S(1)}, bf16[16,96,128]{2,1,0:T(8,128)(2,1)S(1)}, u32[]{:S(2)}, u32[]{:S(2)}) %collective-permute-start.3) | collective-permute-done | bytes 393248 | tf_op jit(solution)/shard_map/ppermute | solution.py:25
  87.3 0.0 copy-done.1
  87.3 4.0 %series.1 = f32[768,128]{1,0:T(8,128)} custom-call(s32[1]{0:T(128)} %bitcast.core_ref.place_ref, bf16[16,96,128]{2,1,0:T(8,128)(2,1)S(1)} %all_to_all.17.own_ref, bf16[16,96,128]{2,1,0:T(8,128)(2,1)S(1)} %collective-permute-done.3.other_ref, f32[768,128]{1,0:T(8,128)S(1)} %bitcast.11), custom_call_target="tpu_custom_call" | custom-call | tf_op jit(solution)/shard_map/series/pallas_call | solution.py:428
  (1 shorter events, 0.0 us)
Async XLA Ops:
  0.6 2.1 %collective-permute-start = (f32[768,128]{1,0:T(8,128)}, f32[768,128]{1,0:T(8,128)S(1)}, u32[]{:S(2)}, u32[]{:S(2)}) collective-permute-start(f32[768,128]{1,0:T(8,128)} %bitcast.9), channel_id=1, source_target_pairs={{0,1},{1,0},{2,3},{3,2},{4,5},{5,4},{6,7},{7,6},{8,9},{9,8},{10,11... | collective-permute-start | bytes 1179656 | tf_op jit(solution)/shard_map/ppermute | solution.py:25
  2.7 1.0 %copy-start = (f32[1,768,128]{2,1,0:T(8,128)S(1)}, f32[1,768,128]{2,1,0:T(8,128)}, u32[]{:S(2)}) copy-start(f32[1,768,128]{2,1,0:T(8,128)} %param.6) | copy-start | bytes 1179652
  3.7 1.1 %copy-start.2 = (f32[768,256]{1,0:T(8,128)S(1)}, f32[768,256]{1,0:T(8,128)}, u32[]{:S(2)}) copy-start(f32[768,256]{1,0:T(8,128)} %trial_ref.1) | copy-start | bytes 2359300
  36.2 4.1 %collective-permute-start.1 = (bf16[16,96,128]{2,1,0:T(8,128)(2,1)S(1)}, bf16[16,96,128]{2,1,0:T(8,128)(2,1)S(1)}, u32[]{:S(2)}, u32[]{:S(2)}) collective-permute-start(bf16[16,96,128]{2,1,0:T(8,128)(2,1)S(1)} %all_to_all.15.green_ref), channel_id=1, source_target_pairs={{0,1},{1,0},{2,3},{3,2},{4,5},{5,4},{6,7},{7,6},{8,9},{9,8},{10,11... | collective-permute-start | bytes 1179656 | tf_op jit(solution)/shard_map/ppermute | solution.py:25
  40.3 18.1 %copy-start.3 = (f32[1,16,256]{2,1,0:T(8,128)S(1)}, f32[1,16,256]{2,1,0:T(8,128)}, u32[]{:S(2)}) copy-start(f32[1,16,256]{2,1,0:T(8,128)} %param.7) | copy-start | bytes 49156
  63.6 23.6 %copy-start.1 = (f32[1,768,128]{2,1,0:T(8,128)S(1)}, f32[1,768,128]{2,1,0:T(8,128)}, u32[]{:S(2)}) copy-start(f32[1,768,128]{2,1,0:T(8,128)} %param.6) | copy-start | bytes 1179652
  63.6 5.1 %collective-permute-start.2 = (f32[96,16,128]{2,0,1:T(8,128)S(1)}, f32[96,16,128]{2,0,1:T(8,128)S(1)}, u32[]{:S(2)}, u32[]{:S(2)}) collective-permute-start(f32[96,16,128]{2,0,1:T(8,128)S(1)} %copy.6), channel_id=1, source_target_pairs={{0,1},{1,0},{2,3},{3,2},{4,5},{5,4},{6,7},{7,6},{8,9},{9,8},{10,11... | collective-permute-start | bytes 2359304 | tf_op jit(solution)/shard_map/ppermute | solution.py:25
  85.5 1.7 %collective-permute-start.3 = (bf16[16,96,128]{2,1,0:T(8,128)(2,1)S(1)}, bf16[16,96,128]{2,1,0:T(8,128)(2,1)S(1)}, u32[]{:S(2)}, u32[]{:S(2)}) collective-permute-start(bf16[16,96,128]{2,1,0:T(8,128)(2,1)S(1)} %all_to_all.17.own_ref), channel_id=1, source_target_pairs={{0,1},{1,0},{2,3},{3,2},{4,5},{5,4},{6,7},{7,6},{8,9},{9,8},{10,11... | collective-permute-start | bytes 1179656 | tf_op jit(solution)/shard_map/ppermute | solution.py:25

commit v3 on v2

--- a/solution.py
+++ b/solution.py
@@ -149,8 +149,8 @@
 
 
 LOW_START = 5e-4
-PAIRED_STEPS = 6
-RESIDUAL_BOUND = 3e-3
+PAIRED_STEPS = 8
+RESIDUAL_BOUND = 1e-2
 MOST_STEPS = 60
 
 
@@ -164,14 +164,41 @@
     return found
 
 
-def green_body(core_ref, own_ref, other_ref, trial_ref, out_ref, inverse_ref, matrix_ref, solved_ref, *, row_groups, col_groups):
+def overlap_body(own_ref, trial_ref, inter_ref, turned_ref):
+    turned_ref[...] = trial_ref[...].T
+    inter_ref[...] = dot_of(turned_ref[...], own_ref[...], precision=highest)
+
+
+def green_body(
+    core_ref, other_ref, inter_ref, trial_turned_ref, own_hbm_ref, trial_hbm_ref, vector_ref,
+    out_ref, kept_ref, inverse_ref, matrix_ref, solved_ref, own_ref, trial_ref, sems,
+    *, row_groups, col_groups
+):
+    early = [
+        pltpu.make_async_copy(own_hbm_ref, own_ref, sems.at[2 * SUBS]),
+        pltpu.make_async_copy(trial_hbm_ref, trial_ref, sems.at[2 * SUBS + 1]),
+    ]
+    for copy in early:
+        copy.start()
+    copies = []
+    for sub in range(SUBS):
+        rows = pl.ds(sub * SUB, SUB)
+        for beside in range(2):
+            cols = pl.ds((sub + beside) % SUBS * SUB, SUB)
+            copies.append(
+                pltpu.make_async_copy(
+                    vector_ref.at[rows, cols, :],
+                    kept_ref.at[rows, pl.ds(beside * SUB, SUB), :],
+                    sems.at[2 * sub + beside],
+                )
+            )
+            copies[-1].start()
     orbital_count, electron_count = trial_ref.shape
     slab_rows = orbital_count // row_groups
     slab_cols = orbital_count // col_groups
     core = core_ref[0]
-    walker = jnp.concatenate([own_ref[...], other_ref[...]], axis=1)
-    trial = trial_ref[...]
-    inter = dot_of(trial, walker, first_dims, highest)
+    inter_other = dot_of(trial_turned_ref[...], other_ref[...], precision=highest)
+    inter = jnp.concatenate([inter_ref[...], inter_other], axis=1)
     inverse_scale = 1.0 / jnp.max(jnp.abs(inter))
     inter = inter * inverse_scale
     matrix_ref[...] = inter
@@ -186,10 +213,11 @@
     scale = step_scales[0]
     error = eye - (2.0 * scale * alpha) * normal + (scale * alpha * alpha) * square
     inverse = (scale * alpha) * (2.0 * turned - alpha * both[:, electron_count:])
-    for scale in step_scales[1:]:
+    for scale in step_scales[1:-1]:
         both = dot_three(error, jnp.concatenate([error, inverse], axis=1))
         inverse = scale * (inverse + both[:, electron_count:])
         error = (1.0 - scale) * eye + scale * both[:, :electron_count]
+    inverse = step_scales[-1] * (inverse + dot_three(error, inverse))
     inverse_ref[...] = inverse
 
     def refine(carried):
@@ -204,6 +232,8 @@
         refine,
         (jnp.int32(0), jnp.float32(1e30)),
     )
+    for copy in early:
+        copy.wait()
     walker_rows = dot_three(
         jnp.concatenate([own_ref[...], other_ref[...]], axis=1), inverse_ref[...]
     )
@@ -233,51 +263,43 @@
                 out_ref[row * col_groups + col, sub * part : (sub + 1) * part, :] = summed[
                     row * part : (row + 1) * part, col * LANES : (col + 1) * LANES
                 ]
-
-
-def bias_body(place_ref, green_ref, same_ref, next_ref, before_ref, out_ref, turned_ref, total_ref):
-    step = pl.program_id(0)
-    block = same_ref.shape[0]
-
-    @pl.when(step == 0)
-    def _():
-        turned_ref[...] = jnp.swapaxes(green_ref[...].astype(f32), 0, 1).astype(bf16)
-        total_ref[...] = before_ref[...]
-
-    left = [turned_ref[step * block + row] for row in range(block)]
-    right = []
-    for row in range(block):
-        right += [same_ref[row], next_ref[row]]
-    total = dot_of(jnp.concatenate(left, axis=1), jnp.concatenate(right, axis=0))
-    total_ref[...] = total_ref[...] + total
-
-    @pl.when(step == pl.num_programs(0) - 1)
-    def _():
-        for device in range(out_ref.shape[0]):
-            out_ref[device] = total_ref[...]
-
-
-def potential_body(place_ref, parts_ref, noise_ref, same_ref, next_ref, bias_ref, out_ref, weights_ref):
-    step = pl.program_id(0)
+    for copy in copies:
+        copy.wait()
+
+
+def kept_rows(kept_ref, sub, place):
+    part = SUB // 2
+    start = pl.multiple_of(sub * SUB + place * part, part)
+    return kept_ref[pl.ds(start, part)].reshape(part * LANES, kept_ref.shape[2])
+
+
+def bias_body(place_ref, green_ref, kept_ref, before_ref, out_ref, turned_ref):
+    part = SUB // 2
+    place = place_ref[0]
+    turned_ref[...] = jnp.swapaxes(green_ref[...].astype(f32), 0, 1).astype(bf16)
+    total = before_ref[...]
+    for sub in range(SUBS):
+        left = [turned_ref[sub * part + row] for row in range(part)]
+        total = total + dot_of(jnp.concatenate(left, axis=1), kept_rows(kept_ref, sub, place))
+    for device in range(out_ref.shape[0]):
+        out_ref[device] = total
+
+
+def potential_body(place_ref, parts_ref, noise_ref, kept_ref, bias_ref, out_ref):
+    part = SUB // 2
+    place = place_ref[0]
     walker_total = noise_ref.shape[0]
-    block = same_ref.shape[0]
-
-    @pl.when(step == 0)
-    def _():
-        bias = parts_ref[0]
-        for device in range(1, parts_ref.shape[0]):
-            bias = bias + parts_ref[device]
-        bias_ref[...] = bias
-        high, low = split_two(noise_ref[...] + root_step * bias)
-        weights_ref[...] = jnp.concatenate([high, low], axis=0)
-
-    right = []
-    for row in range(block):
-        right += [same_ref[row], next_ref[row]]
-    both = dot_of(weights_ref[...], jnp.concatenate(right, axis=0), last_dims)
-    added = both[:walker_total] + both[walker_total:]
-    for row in range(block):
-        out_ref[step * block + row] = added[:, row * LANES : (row + 1) * LANES]
+    bias = parts_ref[0]
+    for device in range(1, parts_ref.shape[0]):
+        bias = bias + parts_ref[device]
+    bias_ref[...] = bias
+    high, low = split_two(noise_ref[...] + root_step * bias)
+    weights = jnp.concatenate([high, low], axis=0)
+    for sub in range(SUBS):
+        both = dot_of(weights, kept_rows(kept_ref, sub, place), last_dims)
+        added = both[:walker_total] + both[walker_total:]
+        for row in range(part):
+            out_ref[sub * part + row] = added[:, row * LANES : (row + 1) * LANES]
 
 
 def series_body(core_ref, own_ref, other_ref, walker_ref, out_ref, matrix_ref, *, row_groups, col_groups):
@@ -327,70 +349,45 @@
 
 smem = pl.BlockSpec(memory_space=pltpu.SMEM)
 vmem = pl.BlockSpec(memory_space=pltpu.VMEM)
-grant = pltpu.CompilerParams(vmem_limit_bytes=16 * 2**20)
-large_grant = pltpu.CompilerParams(vmem_limit_bytes=46 * 2**20)
-
-
-def whole(*shape):
-    return pl.BlockSpec(shape, lambda step, place: (0,) * len(shape))
-
-
-def half_blocks(held, shift):
-    return pl.BlockSpec(
-        (SUB // 2, SUB, held), lambda step, place: (2 * step + place[0], (step + shift) % SUBS, 0)
-    )
-
-
-def bias_half(place, green, vectors, before, copies):
+anywhere = pl.BlockSpec(memory_space=pl.ANY)
+grant = pltpu.CompilerParams(vmem_limit_bytes=20 * 2**20)
+
+
+def bias_half(place, green, kept, before, copies):
     owners, dense, _ = green.shape
-    held = vectors.shape[2]
+    held = kept.shape[2]
     return pl.pallas_call(
         bias_body,
-        grid_spec=pltpu.PrefetchScalarGridSpec(
-            num_scalar_prefetch=1,
-            grid=(SUBS,),
-            in_specs=[
-                whole(owners, dense, LANES),
-                half_blocks(held, 0),
-                half_blocks(held, 1),
-                whole(owners, held),
-            ],
-            out_specs=whole(copies, owners, held),
-            scratch_shapes=[
-                pltpu.VMEM((dense, owners, LANES), bf16),
-                pltpu.VMEM((owners, held), f32),
-            ],
-        ),
+        in_specs=[smem, vmem, vmem, vmem],
+        out_specs=vmem,
+        scratch_shapes=[pltpu.VMEM((dense, owners, LANES), bf16)],
         out_shape=jax.ShapeDtypeStruct((copies, owners, held), f32),
-        compiler_params=large_grant,
+        compiler_params=grant,
         name="bias",
-    )(place, green, vectors, vectors, before)
-
-
-def potential_half(place, parts, noise, vectors):
-    count, owners, held = parts.shape
-    dense = SUBS * SUB // 2
+    )(place, green, in_vmem(kept), before)
+
+
+def in_hbm(value):
+    return pltpu.with_memory_space_constraint(value, pltpu.HBM)
+
+
+def in_vmem(value):
+    return pltpu.with_memory_space_constraint(value, pltpu.VMEM)
+
+
+def potential_half(place, parts, noise, kept):
+    _, owners, held = parts.shape
     return pl.pallas_call(
         potential_body,
-        grid_spec=pltpu.PrefetchScalarGridSpec(
-            num_scalar_prefetch=1,
-            grid=(SUBS,),
-            in_specs=[
-                whole(count, owners, held),
-                whole(owners, held),
-                half_blocks(held, 0),
-                half_blocks(held, 1),
-            ],
-            out_specs=(whole(owners, held), whole(dense, owners, LANES)),
-            scratch_shapes=[pltpu.VMEM((2 * owners, held), bf16)],
-        ),
+        in_specs=[smem, vmem, vmem, vmem],
+        out_specs=(vmem, vmem),
         out_shape=(
             jax.ShapeDtypeStruct((owners, held), f32),
-            jax.ShapeDtypeStruct((dense, owners, LANES), f32),
+            jax.ShapeDtypeStruct((SUBS * SUB // 2, owners, LANES), f32),
         ),
-        compiler_params=large_grant,
+        compiler_params=grant,
         name="potential",
-    )(place, parts, noise, vectors, vectors)
+    )(place, parts, noise, in_vmem(kept))
 
 
 def fast_shards(chol_vectors, trial_orbitals, walkers, field_noise):
@@ -404,24 +401,45 @@
     vectors = jnp.transpose(chol_vectors, (1, 2, 0))
     own = walkers[0]
     other = swapped(own, "walk", 0)
+    inter, trial_turned = pl.pallas_call(
+        overlap_body,
+        out_shape=(
+            jax.ShapeDtypeStruct((electron_count, own.shape[1]), f32),
+            jax.ShapeDtypeStruct((electron_count, orbital_count), f32),
+        ),
+        in_specs=[vmem, vmem],
+        out_specs=(vmem, vmem),
+        compiler_params=grant,
+        name="overlap",
+    )(in_hbm(own), in_hbm(trial_orbitals))
     square = pltpu.VMEM((electron_count, electron_count), f32)
-    outgoing = pl.pallas_call(
+    outgoing, kept = pl.pallas_call(
         functools.partial(green_body, row_groups=row_groups, col_groups=col_groups),
-        out_shape=jax.ShapeDtypeStruct((owners, dense, LANES), bf16),
-        in_specs=[smem, vmem, vmem, vmem],
-        out_specs=vmem,
-        scratch_shapes=[square, square, pltpu.VMEM((orbital_count, electron_count), f32)],
+        out_shape=(
+            jax.ShapeDtypeStruct((owners, dense, LANES), bf16),
+            pltpu.VMEM((SUBS * SUB, LANES, held), bf16),
+        ),
+        in_specs=[smem, vmem, vmem, vmem, anywhere, anywhere, anywhere],
+        out_specs=(vmem, vmem),
+        scratch_shapes=[
+            square,
+            square,
+            pltpu.VMEM((orbital_count, electron_count), f32),
+            pltpu.VMEM(own.shape, f32),
+            pltpu.VMEM(trial_orbitals.shape, f32),
+            pltpu.SemaphoreType.DMA((2 * SUBS + 2,)),
+        ],
         compiler_params=grant,
         name="green",
-    )(core, own, other, trial_orbitals)
+    )(core, other, inter, trial_turned, in_hbm(own), in_hbm(trial_orbitals), in_hbm(vectors))
     axes = ("pairs", "chol")
     arrived = lax.all_to_all(outgoing, axes, split_axis=0, concat_axis=0, tiled=True)
     arrived_other = swapped(arrived, "walk", 0)
-    first = bias_half(core, arrived, vectors, jnp.zeros((owners, held), f32), 1)
-    spread = bias_half(1 - core, arrived_other, vectors, first[0], owners)
+    first = bias_half(core, arrived, kept, jnp.zeros((owners, held), f32), 1)
+    spread = bias_half(1 - core, arrived_other, kept, first[0], owners)
     parts = lax.all_to_all(spread, axes, split_axis=0, concat_axis=0, tiled=True)
-    force_bias, send = potential_half(1 - core, parts, field_noise[0], vectors)
-    _, keep = potential_half(core, parts, field_noise[0], vectors)
+    force_bias, send = potential_half(1 - core, parts, field_noise[0], kept)
+    _, keep = potential_half(core, parts, field_noise[0], kept)
     summed = jnp.swapaxes((keep + swapped(send, "walk", 0)).astype(bf16), 0, 1)
     received = lax.all_to_all(summed, axes, split_axis=0, concat_axis=0, tiled=True)
     received_other = swapped(received, "walk", 0)

time: 91.7 us -> 77.4 us (0.84)
  Pallas kernels: 32.5 us -> 21.6 us
  local copies, waits for them, and re-layouts: 2.4 us -> 0.28 us
    pallas_call x4 -> x5, Pallas kernels: 18.2 us -> 7.81 us  [the longest x2 3.77 us: potential_half(): pl.pallas_call(potential_body, in_specs=[smem, vmem, vmem, vmem], out_spe...]
    unnamed x8 -> x4, local copies, waits for them, and re-layouts: 2.14 us -> 0.01 us
  transfers between devices with their start and end apart: 4 -> 4, of which waited for: 2 -> 3; matrix products, arithmetic and copies ran while one was open for 0% -> 0% of each run, Pallas kernels for 10% -> 6%
where the time goes in v3:
time: 77.4 us; the launch traced here: 77.1 us
  blocking collectives  50.7 us (66%)
  Pallas kernels  21.6 us (28%)
  waiting for transfers between devices  2.88 us (4%)
    all_to_all x1, blocking collectives, fast_shards(): lax.all_to_all(outgoing, axes, split_axis=0, concat_axis=0, tiled=True)  20.9 us
    all_to_all x1, blocking collectives, fast_shards(): lax.all_to_all(summed, axes, split_axis=0, concat_axis=0, tiled=True)  16.2 us
    all_to_all x1, blocking collectives, fast_shards(): lax.all_to_all(spread, axes, split_axis=0, concat_axis=0, tiled=True)  13.6 us
    pallas_call x1, Pallas kernels, fast_shards(): pl.pallas_call(functools.partial(green_body, row_groups=row_groups, col_g...  9.79 us
    pallas_call x1, Pallas kernels, fast_shards(): pl.pallas_call(functools.partial(series_body, row_groups=row_groups, col_...  3.96 us
    pallas_call x2, Pallas kernels, potential_half(): pl.pallas_call(potential_body, in_specs=[smem, vmem, vmem, vmem], out_spe...  3.77 us
    ppermute x4, waiting for transfers between devices, swapped(): return lax.ppermute(value, axis, pairs)  2.88 us
    pallas_call x1, Pallas kernels, fast_shards(): pl.pallas_call(overlap_body, out_shape=(jax.ShapeDtypeStruct((electron_co...  2.12 us
  transfers between devices with their start and end apart: 4, of which 3 were waited for; matrix products, arithmetic and copies ran while one was open for 0% of the time, Pallas kernels for 6%

profile of v3, /device:TPU:0, one launch (start us, length us, event | category | flops | bytes accessed | tf_op | source)
XLA Modules:
  0.0 77.1 jit_solution(15622738911875531663)
XLA Ops:
  0.6 0.6 collective-permute-start
  1.2 2.1 %overlap.1 = (f32[256,128]{1,0:T(8,128)S(1)}, f32[256,768]{1,0:T(8,128)S(1)}) custom-call(f32[768,128]{1,0:T(8,128)} %bitcast.10, f32[768,256]{1,0:T(8,128)} %trial_hbm_ref.1), custom_call_target="tpu_custom_call" | custom-call | tf_op jit(solution)/shard_map/overlap/pallas_call | solution.py:404
  3.3 0.0 collective-permute-done.other_ref
  3.3 9.8 %green.1 = (bf16[16,96,128]{2,1,0:T(8,128)(2,1)S(1)}, bf16[192,128,256]{2,1,0:T(8,128)(2,1)S(1)}) custom-call(s32[1]{0:T(128)} %bitcast.core_ref.place_ref, f32[768,128]{1,0:T(8,128)S(1)} %collective-permute-done.other_ref, f32[256,128]{1,0:T(8,128)S(1)} %get-tuple-element.9.inter_ref, f32[256,768]{1,0:T(8,128)S(1)} %get-tuple-element.10.trial_turned_ref, ...), custom_call_target="tpu_custom_call" | custom-call | tf_op jit(solution)/shard_map/green/pallas_call | solution.py:416
  13.1 0.0 copy-start.1
  13.1 20.9 %all_to_all.15.green_ref = bf16[16,96,128]{2,1,0:T(8,128)(2,1)S(1)} all-to-all(bf16[16,96,128]{2,1,0:T(8,128)(2,1)S(1)} %get-tuple-element.11), channel_id=1, replica_groups=mesh['groups'=1,'pairs'=4,'chol'=4,'walk'=2] {'pairs','chol'}, dimensions={0} | all-to-all | bytes 786432 | tf_op jit(solution)/shard_map/all_to_all | solution.py:436
  34.0 0.0 collective-permute-start.1
  34.0 0.9 %bias.2 = f32[1,16,256]{2,1,0:T(8,128)S(1)} custom-call(s32[1]{0:T(128)} %bitcast.core_ref.place_ref, bf16[16,96,128]{2,1,0:T(8,128)(2,1)S(1)} %all_to_all.15.green_ref, bf16[192,128,256]{2,1,0:T(8,128)(2,1)S(1)} %get-tuple-element.12.kept_ref, f32[16,256]{1,0:T(8,128)S(1)} %broadcast_in_dim.9.before_ref), custom_call_target="tpu_custom_call" | custom-call | tf_op jit(solution)/shard_map/bias/pallas_call | solution.py:359
  35.0 0.8 collective-permute-done.1.green_ref
  35.7 0.0 copy-start
  35.7 1.0 %bias.3 = f32[16,16,256]{2,1,0:T(8,128)S(1)} custom-call(s32[1]{0:T(128)S(6)} %sub.4.place_ref, bf16[16,96,128]{2,1,0:T(8,128)(2,1)S(1)} %collective-permute-done.1.green_ref, bf16[192,128,256]{2,1,0:T(8,128)(2,1)S(1)} %get-tuple-element.12.kept_ref, f32[16,256]{1,0:T(8,128)S(1)} %bitcast.15), custom_call_target="tpu_custom_call" | custom-call | tf_op jit(solution)/shard_map/bias/pallas_call | solution.py:359
  36.7 13.6 %all_to_all.16.parts_ref = f32[16,16,256]{2,1,0:T(8,128)S(1)} all-to-all(f32[16,16,256]{2,1,0:T(8,128)S(1)} %bias.3), channel_id=1, replica_groups=mesh['groups'=1,'pairs'=4,'chol'=4,'walk'=2] {'pairs','chol'}, dimensions={0} | all-to-all | bytes 524288 | tf_op jit(solution)/shard_map/all_to_all | solution.py:440
  50.4 0.0 copy-done.1
  50.4 1.9 %potential.3 = (f32[16,256]{1,0:T(8,128)}, f32[96,16,128]{2,1,0:T(8,128)S(1)}) custom-call(s32[1]{0:T(128)S(6)} %sub.4.place_ref, f32[16,16,256]{2,1,0:T(8,128)S(1)} %all_to_all.16.parts_ref, f32[16,256]{1,0:T(8,128)S(1)} %bitcast.13, bf16[192,128,256]{2,1,0:T(8,128)(2,1)S(1)} %get-tuple-element.12.kept_ref), custom_call_target="tpu_custom_call" | custom-call | tf_op jit(solution)/shard_map/potential/pallas_call | solution.py:380
  52.2 0.3 copy.6
  52.5 0.1 collective-permute-start.2
  52.6 1.9 %potential.2 = (f32[16,256]{1,0:T(8,128)}, f32[96,16,128]{2,1,0:T(8,128)S(1)}) custom-call(s32[1]{0:T(128)} %bitcast.core_ref.place_ref, f32[16,16,256]{2,1,0:T(8,128)S(1)} %all_to_all.16.parts_ref, f32[16,256]{1,0:T(8,128)S(1)} %bitcast.14, bf16[192,128,256]{2,1,0:T(8,128)(2,1)S(1)} %get-tuple-element.12.kept_ref), custom_call_target="tpu_custom_call" | custom-call | tf_op jit(solution)/shard_map/potential/pallas_call | solution.py:380
  54.5 0.4 collective-permute-done.2
  54.9 0.3 fusion.1
  55.1 16.2 %all_to_all.17.own_ref = bf16[16,96,128]{2,1,0:T(8,128)(2,1)S(1)} all-to-all(bf16[16,96,128]{2,1,0:T(8,128)(2,1)S(1)} %fusion.1), channel_id=1, replica_groups=mesh['groups'=1,'pairs'=4,'chol'=4,'walk'=2] {'pairs','chol'}, dimensions={0} | all-to-all | bytes 786432 | tf_op jit(solution)/shard_map/all_to_all | solution.py:444
  71.4 0.0 collective-permute-start.3
  71.4 1.7 %collective-permute-done.3.other_ref = bf16[16,96,128]{2,1,0:T(8,128)(2,1)S(1)} collective-permute-done((bf16[16,96,128]{2,1,0:T(8,128)(2,1)S(1)}, bf16[16,96,128]{2,1,0:T(8,128)(2,1)S(1)}, u32[]{:S(2)}, u32[]{:S(2)}) %collective-permute-start.3) | collective-permute-done | bytes 393248 | tf_op jit(solution)/shard_map/ppermute | solution.py:25
  73.1 0.0 copy-done
  73.1 4.0 %series.1 = f32[768,128]{1,0:T(8,128)} custom-call(s32[1]{0:T(128)} %bitcast.core_ref.place_ref, bf16[16,96,128]{2,1,0:T(8,128)(2,1)S(1)} %all_to_all.17.own_ref, bf16[16,96,128]{2,1,0:T(8,128)(2,1)S(1)} %collective-permute-done.3.other_ref, f32[768,128]{1,0:T(8,128)S(1)} %bitcast.12), custom_call_target="tpu_custom_call" | custom-call | tf_op jit(solution)/shard_map/series/pallas_call | solution.py:446
  (1 shorter events, 0.0 us)
Async XLA Ops:
  0.6 2.7 %collective-permute-start = (f32[768,128]{1,0:T(8,128)}, f32[768,128]{1,0:T(8,128)S(1)}, u32[]{:S(2)}, u32[]{:S(2)}) collective-permute-start(f32[768,128]{1,0:T(8,128)} %bitcast.9), channel_id=1, source_target_pairs={{0,1},{1,0},{2,3},{3,2},{4,5},{5,4},{6,7},{7,6},{8,9},{9,8},{10,11... | collective-permute-start | bytes 1179656 | tf_op jit(solution)/shard_map/ppermute | solution.py:25
  13.1 37.2 %copy-start.1 = (f32[1,16,256]{2,1,0:T(8,128)S(1)}, f32[1,16,256]{2,1,0:T(8,128)}, u32[]{:S(2)}) copy-start(f32[1,16,256]{2,1,0:T(8,128)} %param.7) | copy-start | bytes 49156
  34.0 1.7 %collective-permute-start.1 = (bf16[16,96,128]{2,1,0:T(8,128)(2,1)S(1)}, bf16[16,96,128]{2,1,0:T(8,128)(2,1)S(1)}, u32[]{:S(2)}, u32[]{:S(2)}) collective-permute-start(bf16[16,96,128]{2,1,0:T(8,128)(2,1)S(1)} %all_to_all.15.green_ref), channel_id=1, source_target_pairs={{0,1},{1,0},{2,3},{3,2},{4,5},{5,4},{6,7},{7,6},{8,9},{9,8},{10,11... | collective-permute-start | bytes 1179656 | tf_op jit(solution)/shard_map/ppermute | solution.py:25
  35.7 37.4 %copy-start = (f32[1,768,128]{2,1,0:T(8,128)S(1)}, f32[1,768,128]{2,1,0:T(8,128)}, u32[]{:S(2)}) copy-start(f32[1,768,128]{2,1,0:T(8,128)} %param.6) | copy-start | bytes 1179652
  52.5 2.4 %collective-permute-start.2 = (f32[96,16,128]{2,0,1:T(8,128)S(1)}, f32[96,16,128]{2,0,1:T(8,128)S(1)}, u32[]{:S(2)}, u32[]{:S(2)}) collective-permute-start(f32[96,16,128]{2,0,1:T(8,128)S(1)} %copy.6), channel_id=1, source_target_pairs={{0,1},{1,0},{2,3},{3,2},{4,5},{5,4},{6,7},{7,6},{8,9},{9,8},{10,11... | collective-permute-start | bytes 2359304 | tf_op jit(solution)/shard_map/ppermute | solution.py:25
  71.4 1.7 %collective-permute-start.3 = (bf16[16,96,128]{2,1,0:T(8,128)(2,1)S(1)}, bf16[16,96,128]{2,1,0:T(8,128)(2,1)S(1)}, u32[]{:S(2)}, u32[]{:S(2)}) collective-permute-start(bf16[16,96,128]{2,1,0:T(8,128)(2,1)S(1)} %all_to_all.17.own_ref), channel_id=1, source_target_pairs={{0,1},{1,0},{2,3},{3,2},{4,5},{5,4},{6,7},{7,6},{8,9},{9,8},{10,11... | collective-permute-start | bytes 1179656 | tf_op jit(solution)/shard_map/ppermute | solution.py:25

commit v4 on v3

--- a/solution.py
+++ b/solution.py
@@ -120,13 +120,12 @@
     return lax.dot_general(left, right, dims, precision=precision, preferred_element_type=f32)
 
 
-def dot_three(left, right, dims=(((1,), (0,)), ((), ()))):
+def dot_three(left, right):
     left_high, left_low = split_two(left)
     right_high, right_low = split_two(right)
-    return (
-        dot_of(left_high, right_high, dims)
-        + dot_of(left_high, right_low, dims)
-        + dot_of(left_low, right_high, dims)
+    return dot_of(
+        jnp.concatenate([left_high, left_low, left_high], axis=1),
+        jnp.concatenate([right_high, right_high, right_low], axis=0),
     )
 
 
@@ -164,40 +163,48 @@
     return found
 
 
-def overlap_body(own_ref, trial_ref, inter_ref, turned_ref):
-    turned_ref[...] = trial_ref[...].T
-    inter_ref[...] = dot_of(turned_ref[...], own_ref[...], precision=highest)
+def three_terms(left, right, dims=(((1,), (0,)), ((), ()))):
+    count = left[0].shape[0]
+    both = dot_of(jnp.concatenate(left, axis=0), right[0], dims)
+    return both[:count] + both[count:] + dot_of(left[0], right[1], dims)
+
+
+def overlap_body(own_ref, trial_ref, inter_ref, turned_high_ref, turned_low_ref, high_ref, low_ref, own_high_ref, own_low_ref):
+    trial = trial_ref[...]
+    own = split_two(own_ref[...])
+    turned = split_two(trial.T)
+    inter_ref[...] = three_terms(turned, own)
+    turned_high_ref[...], turned_low_ref[...] = turned
+    high_ref[...], low_ref[...] = split_two(trial)
+    own_high_ref[...], own_low_ref[...] = own
 
 
 def green_body(
-    core_ref, other_ref, inter_ref, trial_turned_ref, own_hbm_ref, trial_hbm_ref, vector_ref,
-    out_ref, kept_ref, inverse_ref, matrix_ref, solved_ref, own_ref, trial_ref, sems,
-    *, row_groups, col_groups
+    core_ref, other_ref, inter_ref, turned_high_ref, turned_low_ref, high_ref, low_ref, own_high_ref,
+    own_low_ref, vector_ref, out_ref, kept_ref, inverse_ref, matrix_ref,
+    solved_high_ref, solved_low_ref, sems, *, row_groups, col_groups
 ):
-    early = [
-        pltpu.make_async_copy(own_hbm_ref, own_ref, sems.at[2 * SUBS]),
-        pltpu.make_async_copy(trial_hbm_ref, trial_ref, sems.at[2 * SUBS + 1]),
-    ]
-    for copy in early:
-        copy.start()
+    core = core_ref[0]
+    odd = core_ref[1]
     copies = []
     for sub in range(SUBS):
         rows = pl.ds(sub * SUB, SUB)
         for beside in range(2):
             cols = pl.ds((sub + beside) % SUBS * SUB, SUB)
+            target = odd if beside == 0 else 1 - odd
             copies.append(
                 pltpu.make_async_copy(
                     vector_ref.at[rows, cols, :],
-                    kept_ref.at[rows, pl.ds(beside * SUB, SUB), :],
+                    kept_ref.at[rows, pl.ds(pl.multiple_of(target * SUB, SUB), SUB), :],
                     sems.at[2 * sub + beside],
                 )
             )
             copies[-1].start()
-    orbital_count, electron_count = trial_ref.shape
+    orbital_count, electron_count = high_ref.shape
     slab_rows = orbital_count // row_groups
     slab_cols = orbital_count // col_groups
-    core = core_ref[0]
-    inter_other = dot_of(trial_turned_ref[...], other_ref[...], precision=highest)
+    other = split_two(other_ref[...])
+    inter_other = three_terms((turned_high_ref[...], turned_low_ref[...]), other)
     inter = jnp.concatenate([inter_ref[...], inter_other], axis=1)
     inverse_scale = 1.0 / jnp.max(jnp.abs(inter))
     inter = inter * inverse_scale
@@ -217,13 +224,12 @@
         both = dot_three(error, jnp.concatenate([error, inverse], axis=1))
         inverse = scale * (inverse + both[:, electron_count:])
         error = (1.0 - scale) * eye + scale * both[:, :electron_count]
-    inverse = step_scales[-1] * (inverse + dot_three(error, inverse))
-    inverse_ref[...] = inverse
+    inverse_ref[...] = step_scales[-1] * (inverse + dot_three(error, inverse))
 
     def refine(carried):
         count, _ = carried
         current = inverse_ref[...]
-        residual = eye_of(electron_count) - dot_of(current, matrix_ref[...], precision=highest)
+        residual = eye_of(electron_count) - dot_three(current, matrix_ref[...])
         inverse_ref[...] = current + dot_three(residual, current)
         return count + 1, jnp.sum(residual * residual)
 
@@ -232,36 +238,46 @@
         refine,
         (jnp.int32(0), jnp.float32(1e30)),
     )
-    for copy in early:
-        copy.wait()
-    walker_rows = dot_three(
-        jnp.concatenate([own_ref[...], other_ref[...]], axis=1), inverse_ref[...]
-    )
-    solved_ref[...] = walker_rows * inverse_scale
+    walker = [
+        jnp.concatenate([own, there], axis=1)
+        for own, there in zip((own_high_ref[...], own_low_ref[...]), other)
+    ]
+    inverse = inverse_ref[...] * inverse_scale
+    solved_high_ref[...], solved_low_ref[...] = split_two(three_terms(walker, split_two(inverse)))
     part = SUB // 2
-    empty = jnp.zeros((SUB, electron_count), f32)
+    trial_refs = (high_ref, low_ref)
+    solved_refs = (solved_high_ref, solved_low_ref)
     for sub in range(SUBS):
         following = (sub + 1) % SUBS
         starts = [
-            pl.multiple_of(row * slab_rows + sub * SUB + core * part, 8) for row in range(row_groups)
+            pl.multiple_of(row * slab_rows + sub * SUB + core * part, part) for row in range(row_groups)
         ]
-        left = jnp.concatenate([solved_ref[pl.ds(start, part), :] for start in starts], axis=0)
-        left_turned = jnp.concatenate([trial_ref[pl.ds(start, part), :] for start in starts], axis=0)
-        right = []
-        right_turned = []
+        same = [col * slab_cols + sub * SUB for col in range(col_groups)]
+        beside = [col * slab_cols + following * SUB for col in range(col_groups)]
+        mixed = []
         for col in range(col_groups):
-            same = col * slab_cols + sub * SUB
-            next_one = col * slab_cols + following * SUB
-            right += [trial_ref[same : same + SUB, :], trial_ref[next_one : next_one + SUB, :]]
-            right_turned += [empty, solved_ref[next_one : next_one + SUB, :]]
-        green = dot_three(left, jnp.concatenate(right, axis=0), last_dims)
-        turned = dot_three(left_turned, jnp.concatenate(right_turned, axis=0), last_dims)
-        summed = green.astype(bf16).astype(f32) + turned.astype(bf16).astype(f32)
-        summed = summed.astype(bf16)
-        for row in range(row_groups):
-            for col in range(col_groups):
+            mixed += [beside[col], same[col]] if col % 2 else [same[col], beside[col]]
+
+        def rows_of(refs, places, size):
+            return [jnp.concatenate([ref[pl.ds(at, size), :] for at in places], axis=0) for ref in refs]
+
+        green = three_terms(
+            rows_of(solved_refs, starts, part), rows_of(trial_refs, mixed, SUB), last_dims
+        )
+        turned = three_terms(
+            rows_of(trial_refs, starts, part), rows_of(solved_refs, beside, SUB), last_dims
+        )
+        for col in range(col_groups):
+            tile = green[:, col * LANES : (col + 1) * LANES].astype(bf16).astype(f32)
+            lane = col // 2 * LANES
+            added = half_rolled(turned[:, lane : lane + LANES]).astype(bf16).astype(f32)
+            first = tail_lanes(tile)
+            plain, summed = tile, tile + added
+            summed = jnp.where(first, summed, plain) if col % 2 else jnp.where(first, plain, summed)
+            summed = summed.astype(bf16)
+            for row in range(row_groups):
                 out_ref[row * col_groups + col, sub * part : (sub + 1) * part, :] = summed[
-                    row * part : (row + 1) * part, col * LANES : (col + 1) * LANES
+                    row * part : (row + 1) * part
                 ]
     for copy in copies:
         copy.wait()
@@ -302,32 +318,47 @@
             out_ref[sub * part + row] = added[:, row * LANES : (row + 1) * LANES]
 
 
-def series_body(core_ref, own_ref, other_ref, walker_ref, out_ref, matrix_ref, *, row_groups, col_groups):
+def joined_tiles(source_ref, sub, row, col_groups):
+    part = SUB // 2
+    same = []
+    beside = []
+    for col in range(0, col_groups, 2):
+        index = row * col_groups + col
+        even = source_ref[index, sub * part : (sub + 1) * part, :]
+        odd = source_ref[index + 1, sub * part : (sub + 1) * part, :]
+        same.append(jnp.where(tail_lanes(even), even, odd))
+        beside.append(half_rolled(jnp.where(tail_lanes(even), odd, even).astype(f32)).astype(bf16))
+    return jnp.concatenate(same + beside, axis=1)
+
+
+def joined_body(source_ref, out_ref, *, row_groups, col_groups):
+    for sub in range(SUBS):
+        for row in range(row_groups):
+            out_ref[sub * row_groups + row] = joined_tiles(source_ref, sub, row, col_groups)
+
+
+def series_body(core_ref, joined_ref, other_ref, walker_ref, out_ref, matrix_ref, stage_ref, sems, *, row_groups, col_groups):
     slab = SUB * SUBS
     part = SUB // 2
     size = row_groups * SUB
     core = core_ref[0]
-    for source, place in ((own_ref, core), (other_ref, 1 - core)):
+    for place in range(2):
         for sub in range(SUBS):
-            following = (sub + 1) % SUBS
+            lane = (sub + 1) % SUBS * size
             for row in range(row_groups):
-                start = pl.multiple_of(sub * size + row * SUB + place * part, 16)
-                for col in range(0, col_groups, 2):
-                    index = row * col_groups + col
-                    even = source[index, sub * part : (sub + 1) * part, :].astype(f32)
-                    odd = source[index + 1, sub * part : (sub + 1) * part, :].astype(f32)
-                    same = jnp.where(tail_lanes(even), even, half_rolled(odd)).astype(bf16)
-                    beside = jnp.where(tail_lanes(even), half_rolled(even), odd).astype(bf16)
-                    lane = col // 2 * LANES
-                    matrix_ref[pl.ds(start, part), sub * size + lane : sub * size + lane + LANES] = same
-                    lane += following * size
-                    matrix_ref[pl.ds(start, part), lane : lane + LANES] = beside
+                if place == 0:
+                    tiles = joined_ref[sub * row_groups + row]
+                    shift = core * part
+                else:
+                    tiles = joined_tiles(other_ref, sub, row, col_groups)
+                    shift = (1 - core) * part
+                rows = pl.ds(pl.multiple_of(sub * size + row * SUB + shift, part), part)
+                matrix_ref[rows, sub * size : (sub + 1) * size] = tiles[:, :size]
+                matrix_ref[rows, lane : lane + size] = tiles[:, size:]
     for sub in range(SUBS):
         following = (sub + 1) % SUBS
         block = matrix_ref[sub * size : (sub + 1) * size, following * size : (following + 1) * size]
-        matrix_ref[following * size : (following + 1) * size, sub * size : (sub + 1) * size] = (
-            block.astype(f32).T.astype(bf16)
-        )
+        matrix_ref[following * size : (following + 1) * size, sub * size : (sub + 1) * size] = block.T
 
     pieces = []
     for sub in range(SUBS):
@@ -336,15 +367,29 @@
     term = jnp.concatenate(pieces, axis=0)
     total = term
     width = term.shape[1]
-    for degree in range(1, TERMS):
-        high, low = split_two(term)
-        both = dot_of(matrix_ref[...], jnp.concatenate([high, low], axis=1))
+    for degree in range(1, TERMS - 1):
+        right = jnp.concatenate(split_two(term), axis=1)
+        both = dot_of(matrix_ref[...], right)
         term = (-root_step / degree) * (both[:, :width] + both[:, width:])
         total = total + term
-    for sub in range(SUBS):
+    right = jnp.concatenate(split_two(term), axis=1)
+    copies = []
+    for sub in range(SUBS):
+        rows = slice(sub * size, (sub + 1) * size)
+        both = dot_of(matrix_ref[rows, :], right)
+        term = (-root_step / (TERMS - 1)) * (both[:, :width] + both[:, width:])
+        stage_ref[rows, :] = total[rows] + term
         for row in range(row_groups):
-            start = sub * size + row * SUB
-            out_ref[row * slab + sub * SUB : row * slab + (sub + 1) * SUB, :] = total[start : start + SUB]
+            copies.append(
+                pltpu.make_async_copy(
+                    stage_ref.at[pl.ds(sub * size + row * SUB, SUB), :],
+                    out_ref.at[pl.ds(row * slab + sub * SUB, SUB), :],
+                    sems.at[sub * row_groups + row],
+                )
+            )
+            copies[-1].start()
+    for copy in copies:
+        copy.wait()
 
 
 smem = pl.BlockSpec(memory_space=pltpu.SMEM)
@@ -398,40 +443,40 @@
     owners = row_groups * col_groups
     dense = SUBS * SUB // 2
     core = lax.axis_index("walk").astype(jnp.int32).reshape(1)
+    parity = (lax.axis_index("chol").astype(jnp.int32) % 2).reshape(1)
     vectors = jnp.transpose(chol_vectors, (1, 2, 0))
     own = walkers[0]
     other = swapped(own, "walk", 0)
-    inter, trial_turned = pl.pallas_call(
+    early = pl.pallas_call(
         overlap_body,
-        out_shape=(
-            jax.ShapeDtypeStruct((electron_count, own.shape[1]), f32),
-            jax.ShapeDtypeStruct((electron_count, orbital_count), f32),
-        ),
+        out_shape=[jax.ShapeDtypeStruct((electron_count, own.shape[1]), f32)]
+        + [jax.ShapeDtypeStruct((electron_count, orbital_count), bf16)] * 2
+        + [jax.ShapeDtypeStruct(trial_orbitals.shape, bf16)] * 2
+        + [jax.ShapeDtypeStruct(own.shape, bf16)] * 2,
         in_specs=[vmem, vmem],
-        out_specs=(vmem, vmem),
+        out_specs=[vmem] * 7,
         compiler_params=grant,
         name="overlap",
     )(in_hbm(own), in_hbm(trial_orbitals))
-    square = pltpu.VMEM((electron_count, electron_count), f32)
+    square = (electron_count, electron_count)
     outgoing, kept = pl.pallas_call(
         functools.partial(green_body, row_groups=row_groups, col_groups=col_groups),
         out_shape=(
             jax.ShapeDtypeStruct((owners, dense, LANES), bf16),
             pltpu.VMEM((SUBS * SUB, LANES, held), bf16),
         ),
-        in_specs=[smem, vmem, vmem, vmem, anywhere, anywhere, anywhere],
+        in_specs=[smem] + [vmem] * 8 + [anywhere],
         out_specs=(vmem, vmem),
         scratch_shapes=[
-            square,
-            square,
-            pltpu.VMEM((orbital_count, electron_count), f32),
-            pltpu.VMEM(own.shape, f32),
-            pltpu.VMEM(trial_orbitals.shape, f32),
-            pltpu.SemaphoreType.DMA((2 * SUBS + 2,)),
+            pltpu.VMEM(square, f32),
+            pltpu.VMEM(square, f32),
+            pltpu.VMEM(trial_orbitals.shape, bf16),
+            pltpu.VMEM(trial_orbitals.shape, bf16),
+            pltpu.SemaphoreType.DMA((2 * SUBS,)),
         ],
         compiler_params=grant,
         name="green",
-    )(core, other, inter, trial_turned, in_hbm(own), in_hbm(trial_orbitals), in_hbm(vectors))
+    )(jnp.concatenate([core, parity]), other, *early, in_hbm(vectors))
     axes = ("pairs", "chol")
     arrived = lax.all_to_all(outgoing, axes, split_axis=0, concat_axis=0, tiled=True)
     arrived_other = swapped(arrived, "walk", 0)
@@ -443,15 +488,28 @@
     summed = jnp.swapaxes((keep + swapped(send, "walk", 0)).astype(bf16), 0, 1)
     received = lax.all_to_all(summed, axes, split_axis=0, concat_axis=0, tiled=True)
     received_other = swapped(received, "walk", 0)
+    sizes = dict(row_groups=row_groups, col_groups=col_groups)
+    joined = pl.pallas_call(
+        functools.partial(joined_body, **sizes),
+        out_shape=jax.ShapeDtypeStruct((SUBS * row_groups, SUB // 2, 2 * SUB * col_groups), bf16),
+        in_specs=[vmem],
+        out_specs=vmem,
+        compiler_params=grant,
+        name="joined",
+    )(received)
     propagated = pl.pallas_call(
-        functools.partial(series_body, row_groups=row_groups, col_groups=col_groups),
+        functools.partial(series_body, **sizes),
         out_shape=jax.ShapeDtypeStruct(own.shape, f32),
         in_specs=[smem, vmem, vmem, vmem],
-        out_specs=vmem,
-        scratch_shapes=[pltpu.VMEM((orbital_count, orbital_count), bf16)],
+        out_specs=anywhere,
+        scratch_shapes=[
+            pltpu.VMEM((orbital_count, orbital_count), bf16),
+            pltpu.VMEM(own.shape, f32),
+            pltpu.SemaphoreType.DMA((SUBS * row_groups,)),
+        ],
         compiler_params=grant,
         name="series",
-    )(core, received, received_other, own)
+    )(core, joined, received_other, own)
     return propagated[None], force_bias[None]
 
 

time: 77.4 us -> 74.9 us (0.968)
  Pallas kernels: 21.6 us -> 18.9 us
    pallas_call x1, Pallas kernels: 9.79 us -> 7.55 us  [fast_shards(): pl.pallas_call(functools.partial(green_body, row_groups=row_groups, col_g...]
    pallas_call x2 -> x3, Pallas kernels: 6.08 us -> 5.68 us  [the longest x1 3.75 us: fast_shards(): pl.pallas_call(functools.partial(series_body, **sizes), out_shape=jax.Sha...]
where the time goes in v4:
time: 74.9 us; the launch traced here: 74.6 us
  blocking collectives  50.9 us (68%)
  Pallas kernels  18.9 us (25%)
  waiting for transfers between devices  2.75 us (4%)
    all_to_all x1, blocking collectives, fast_shards(): lax.all_to_all(outgoing, axes, split_axis=0, concat_axis=0, tiled=True)  20.9 us
    all_to_all x1, blocking collectives, fast_shards(): lax.all_to_all(summed, axes, split_axis=0, concat_axis=0, tiled=True)  16.2 us
    all_to_all x1, blocking collectives, fast_shards(): lax.all_to_all(spread, axes, split_axis=0, concat_axis=0, tiled=True)  13.7 us
    pallas_call x1, Pallas kernels, fast_shards(): pl.pallas_call(functools.partial(green_body, row_groups=row_groups, col_g...  7.55 us
    pallas_call x2, Pallas kernels, potential_half(): pl.pallas_call(potential_body, in_specs=[smem, vmem, vmem, vmem], out_spe...  3.78 us
    pallas_call x1, Pallas kernels, fast_shards(): pl.pallas_call(functools.partial(series_body, **sizes), out_shape=jax.Sha...  3.75 us
    ppermute x4, waiting for transfers between devices, swapped(): return lax.ppermute(value, axis, pairs)  2.75 us
    pallas_call x2, Pallas kernels, bias_half(): pl.pallas_call(bias_body, in_specs=[smem, vmem, vmem, vmem], out_specs=vm...  1.93 us
  transfers between devices with their start and end apart: 4, of which 3 were waited for; matrix products, arithmetic and copies ran while one was open for 0% of the time, Pallas kernels for 6%

profile of v4, /device:TPU:0, one launch (start us, length us, event | category | flops | bytes accessed | tf_op | source)
XLA Modules:
  0.0 74.6 jit_solution(12198180096056255846)
XLA Ops:
  0.6 0.6 collective-permute-start
  1.2 1.8 %overlap.1 = (f32[256,128]{1,0:T(8,128)S(1)}, bf16[256,768]{1,0:T(8,128)(2,1)S(1)}, bf16[256,768]{1,0:T(8,128)(2,1)S(1)}, bf16[768,256]{1,0:T(8,128)(2,1)S(1)}, ...) custom-call(f32[768,128]{1,0:T(8,128)} %bitcast.11, f32[768,256]{1,0:T(8,128)} %trial_ref.1), custom_call_target="tpu_custom_call" | custom-call | tf_op jit(solution)/shard_map/overlap/pallas_call | solution.py:450
  3.0 0.1 pad_add_fusion.core_ref
  3.1 0.0 collective-permute-done.other_ref
  3.1 7.6 %green.1 = (bf16[16,96,128]{2,1,0:T(8,128)(2,1)S(1)}, bf16[192,128,256]{2,1,0:T(8,128)(2,1)S(1)}) custom-call(s32[2]{0:T(128)S(1)} %pad_add_fusion.core_ref, f32[768,128]{1,0:T(8,128)S(1)} %collective-permute-done.other_ref, f32[256,128]{1,0:T(8,128)S(1)} %get-tuple-element.14.inter_ref, bf16[256,768]{1,0:T(8,128)(2,1)S(1)} %get-tuple-element.15.turned_high_ref, ...), custom_call_target="tpu_custom_call" | custom-call | tf_op jit(solution)/shard_map/green/pallas_call | solution.py:462
  10.6 0.0 copy-start.1
  10.7 20.9 %all_to_all.15.green_ref = bf16[16,96,128]{2,1,0:T(8,128)(2,1)S(1)} all-to-all(bf16[16,96,128]{2,1,0:T(8,128)(2,1)S(1)} %get-tuple-element.21), channel_id=1, replica_groups=mesh['groups'=1,'pairs'=4,'chol'=4,'walk'=2] {'pairs','chol'}, dimensions={0} | all-to-all | bytes 786432 | tf_op jit(solution)/shard_map/all_to_all | solution.py:481
  31.6 0.0 collective-permute-start.1
  31.6 0.9 %bias.2 = f32[1,16,256]{2,1,0:T(8,128)S(1)} custom-call(s32[1]{0:T(128)} %bitcast.place_ref.core_ref, bf16[16,96,128]{2,1,0:T(8,128)(2,1)S(1)} %all_to_all.15.green_ref, bf16[192,128,256]{2,1,0:T(8,128)(2,1)S(1)} %get-tuple-element.22.kept_ref, f32[16,256]{1,0:T(8,128)S(1)} %broadcast_in_dim.9.before_ref), custom_call_target="tpu_custom_call" | custom-call | tf_op jit(solution)/shard_map/bias/pallas_call | solution.py:404
  32.5 0.8 %collective-permute-done.1.green_ref = bf16[16,96,128]{2,1,0:T(8,128)(2,1)S(1)} collective-permute-done((bf16[16,96,128]{2,1,0:T(8,128)(2,1)S(1)}, bf16[16,96,128]{2,1,0:T(8,128)(2,1)S(1)}, u32[]{:S(2)}, u32[]{:S(2)}) %collective-permute-start.1) | collective-permute-done | bytes 393248 | tf_op jit(solution)/shard_map/ppermute | solution.py:25
  33.3 1.0 %bias.3 = f32[16,16,256]{2,1,0:T(8,128)S(1)} custom-call(s32[1]{0:T(128)S(6)} %sub.4.place_ref, bf16[16,96,128]{2,1,0:T(8,128)(2,1)S(1)} %collective-permute-done.1.green_ref, bf16[192,128,256]{2,1,0:T(8,128)(2,1)S(1)} %get-tuple-element.22.kept_ref, f32[16,256]{1,0:T(8,128)S(1)} %bitcast.15), custom_call_target="tpu_custom_call" | custom-call | tf_op jit(solution)/shard_map/bias/pallas_call | solution.py:404
  34.3 0.0 copy-start
  34.3 13.7 %all_to_all.16.parts_ref = f32[16,16,256]{2,1,0:T(8,128)S(1)} all-to-all(f32[16,16,256]{2,1,0:T(8,128)S(1)} %bias.3), channel_id=1, replica_groups=mesh['groups'=1,'pairs'=4,'chol'=4,'walk'=2] {'pairs','chol'}, dimensions={0} | all-to-all | bytes 524288 | tf_op jit(solution)/shard_map/all_to_all | solution.py:485
  48.0 0.0 copy-done.1
  48.1 1.9 %potential.3 = (f32[16,256]{1,0:T(8,128)}, f32[96,16,128]{2,1,0:T(8,128)S(1)}) custom-call(s32[1]{0:T(128)S(6)} %sub.4.place_ref, f32[16,16,256]{2,1,0:T(8,128)S(1)} %all_to_all.16.parts_ref, f32[16,256]{1,0:T(8,128)S(1)} %bitcast.13, bf16[192,128,256]{2,1,0:T(8,128)(2,1)S(1)} %get-tuple-element.22.kept_ref), custom_call_target="tpu_custom_call" | custom-call | tf_op jit(solution)/shard_map/potential/pallas_call | solution.py:425
  49.9 0.3 copy.6
  50.2 0.1 collective-permute-start.2
  50.3 1.9 %potential.2 = (f32[16,256]{1,0:T(8,128)}, f32[96,16,128]{2,1,0:T(8,128)S(1)}) custom-call(s32[1]{0:T(128)} %bitcast.place_ref.core_ref, f32[16,16,256]{2,1,0:T(8,128)S(1)} %all_to_all.16.parts_ref, f32[16,256]{1,0:T(8,128)S(1)} %bitcast.14, bf16[192,128,256]{2,1,0:T(8,128)(2,1)S(1)} %get-tuple-element.22.kept_ref), custom_call_target="tpu_custom_call" | custom-call | tf_op jit(solution)/shard_map/potential/pallas_call | solution.py:425
  52.2 0.4 collective-permute-done.2
  52.6 0.3 fusion.1
  52.8 16.2 %all_to_all.17.source_ref = bf16[16,96,128]{2,1,0:T(8,128)(2,1)S(1)} all-to-all(bf16[16,96,128]{2,1,0:T(8,128)(2,1)S(1)} %fusion.1), channel_id=1, replica_groups=mesh['groups'=1,'pairs'=4,'chol'=4,'walk'=2] {'pairs','chol'}, dimensions={0} | all-to-all | bytes 786432 | tf_op jit(solution)/shard_map/all_to_all | solution.py:489
  69.1 0.0 collective-permute-start.3
  69.1 0.1 joined.1.joined_ref
  69.2 1.6 %collective-permute-done.3.other_ref = bf16[16,96,128]{2,1,0:T(8,128)(2,1)S(1)} collective-permute-done((bf16[16,96,128]{2,1,0:T(8,128)(2,1)S(1)}, bf16[16,96,128]{2,1,0:T(8,128)(2,1)S(1)}, u32[]{:S(2)}, u32[]{:S(2)}) %collective-permute-start.3) | collective-permute-done | bytes 393248 | tf_op jit(solution)/shard_map/ppermute | solution.py:25
  70.8 0.0 copy-done
  70.8 3.7 %series.1 = f32[768,128]{1,0:T(8,128)} custom-call(s32[1]{0:T(128)} %bitcast.place_ref.core_ref, bf16[12,32,512]{2,1,0:T(8,128)(2,1)S(1)} %joined.1.joined_ref, bf16[16,96,128]{2,1,0:T(8,128)(2,1)S(1)} %collective-permute-done.3.other_ref, f32[768,128]{1,0:T(8,128)S(1)} %bitcast.12), custom_call_target="tpu_custom_call" | custom-call | tf_op jit(solution)/shard_map/series/pallas_call | solution.py:500
  (1 shorter events, 0.0 us)
Async XLA Ops:
  0.6 2.5 %collective-permute-start = (f32[768,128]{1,0:T(8,128)}, f32[768,128]{1,0:T(8,128)S(1)}, u32[]{:S(2)}, u32[]{:S(2)}) collective-permute-start(f32[768,128]{1,0:T(8,128)} %bitcast.10), channel_id=1, source_target_pairs={{0,1},{1,0},{2,3},{3,2},{4,5},{5,4},{6,7},{7,6},{8,9},{9,8},{10,11... | collective-permute-start | bytes 1179656 | tf_op jit(solution)/shard_map/ppermute | solution.py:25
  10.6 37.4 %copy-start.1 = (f32[1,16,256]{2,1,0:T(8,128)S(1)}, f32[1,16,256]{2,1,0:T(8,128)}, u32[]{:S(2)}) copy-start(f32[1,16,256]{2,1,0:T(8,128)} %param.7) | copy-start | bytes 49156
  31.6 1.7 %collective-permute-start.1 = (bf16[16,96,128]{2,1,0:T(8,128)(2,1)S(1)}, bf16[16,96,128]{2,1,0:T(8,128)(2,1)S(1)}, u32[]{:S(2)}, u32[]{:S(2)}) collective-permute-start(bf16[16,96,128]{2,1,0:T(8,128)(2,1)S(1)} %all_to_all.15.green_ref), channel_id=1, source_target_pairs={{0,1},{1,0},{2,3},{3,2},{4,5},{5,4},{6,7},{7,6},{8,9},{9,8},{10,11... | collective-permute-start | bytes 1179656 | tf_op jit(solution)/shard_map/ppermute | solution.py:25
  34.3 36.5 %copy-start = (f32[1,768,128]{2,1,0:T(8,128)S(1)}, f32[1,768,128]{2,1,0:T(8,128)}, u32[]{:S(2)}) copy-start(f32[1,768,128]{2,1,0:T(8,128)} %param.6) | copy-start | bytes 1179652
  50.2 2.4 %collective-permute-start.2 = (f32[96,16,128]{2,0,1:T(8,128)S(1)}, f32[96,16,128]{2,0,1:T(8,128)S(1)}, u32[]{:S(2)}, u32[]{:S(2)}) collective-permute-start(f32[96,16,128]{2,0,1:T(8,128)S(1)} %copy.6), channel_id=1, source_target_pairs={{0,1},{1,0},{2,3},{3,2},{4,5},{5,4},{6,7},{7,6},{8,9},{9,8},{10,11... | collective-permute-start | bytes 2359304 | tf_op jit(solution)/shard_map/ppermute | solution.py:25
  69.1 1.7 %collective-permute-start.3 = (bf16[16,96,128]{2,1,0:T(8,128)(2,1)S(1)}, bf16[16,96,128]{2,1,0:T(8,128)(2,1)S(1)}, u32[]{:S(2)}, u32[]{:S(2)}) collective-permute-start(bf16[16,96,128]{2,1,0:T(8,128)(2,1)S(1)} %all_to_all.17.source_ref), channel_id=1, source_target_pairs={{0,1},{1,0},{2,3},{3,2},{4,5},{5,4},{6,7},{7,6},{8,9},{9,8},{10,11... | collective-permute-start | bytes 1179656 | tf_op jit(solution)/shard_map/ppermute | solution.py:25

commit v5 on v4

--- a/solution.py
+++ b/solution.py
@@ -147,9 +147,9 @@
     return lax.broadcasted_iota(jnp.int32, value.shape, 1) < LANES // 2
 
 
-LOW_START = 5e-4
-PAIRED_STEPS = 8
-RESIDUAL_BOUND = 1e-2
+LOW_START = 4e-4
+PAIRED_STEPS = 7
+RESIDUAL_BOUND = 2e-2
 MOST_STEPS = 60
 
 
@@ -364,21 +364,22 @@
     for sub in range(SUBS):
         for row in range(row_groups):
             pieces.append(walker_ref[row * slab + sub * SUB : row * slab + (sub + 1) * SUB, :])
-    term = jnp.concatenate(pieces, axis=0)
+    term = jnp.concatenate(pieces, axis=0).T
     total = term
-    width = term.shape[1]
-    for degree in range(1, TERMS - 1):
-        right = jnp.concatenate(split_two(term), axis=1)
-        both = dot_of(matrix_ref[...], right)
-        term = (-root_step / degree) * (both[:, :width] + both[:, width:])
+    count = term.shape[0]
+    for degree in range(1, TERMS):
+        pair = split_two(term)
+        if degree < 3:
+            both = dot_of(jnp.concatenate(pair, axis=0), matrix_ref[...])
+            both = both[:count] + both[count:]
+        else:
+            both = dot_of(pair[0], matrix_ref[...])
+        term = (-root_step / degree) * both
         total = total + term
-    right = jnp.concatenate(split_two(term), axis=1)
     copies = []
     for sub in range(SUBS):
         rows = slice(sub * size, (sub + 1) * size)
-        both = dot_of(matrix_ref[rows, :], right)
-        term = (-root_step / (TERMS - 1)) * (both[:, :width] + both[:, width:])
-        stage_ref[rows, :] = total[rows] + term
+        stage_ref[rows, :] = total[:, rows].T
         for row in range(row_groups):
             copies.append(
                 pltpu.make_async_copy(

time: 74.9 us -> 73.4 us (0.980)
  Pallas kernels: 18.9 us -> 17.5 us
    pallas_call x1, Pallas kernels: 3.75 us -> 2.66 us  [fast_shards(): pl.pallas_call(functools.partial(series_body, **sizes), out_shape=jax.Sha...]
  transfers between devices with their start and end apart: 4 -> 4, of which waited for: 3 -> 3; matrix products, arithmetic and copies ran while one was open for 0% -> 0% of each run, Pallas kernels for 6% -> 7%
where the time goes in v5:
time: 73.4 us; the launch traced here: 73.1 us
  blocking collectives  50.9 us (69%)
  Pallas kernels  17.5 us (24%)
  waiting for transfers between devices  2.74 us (4%)
    all_to_all x1, blocking collectives, fast_shards(): lax.all_to_all(outgoing, axes, split_axis=0, concat_axis=0, tiled=True)  20.9 us
    all_to_all x1, blocking collectives, fast_shards(): lax.all_to_all(summed, axes, split_axis=0, concat_axis=0, tiled=True)  16.2 us
    all_to_all x1, blocking collectives, fast_shards(): lax.all_to_all(spread, axes, split_axis=0, concat_axis=0, tiled=True)  13.7 us
    pallas_call x1, Pallas kernels, fast_shards(): pl.pallas_call(functools.partial(green_body, row_groups=row_groups, col_g...  7.21 us
    pallas_call x2, Pallas kernels, potential_half(): pl.pallas_call(potential_body, in_specs=[smem, vmem, vmem, vmem], out_spe...  3.78 us
    ppermute x4, waiting for transfers between devices, swapped(): return lax.ppermute(value, axis, pairs)  2.74 us
    pallas_call x1, Pallas kernels, fast_shards(): pl.pallas_call(functools.partial(series_body, **sizes), out_shape=jax.Sha...  2.66 us
    pallas_call x2, Pallas kernels, bias_half(): pl.pallas_call(bias_body, in_specs=[smem, vmem, vmem, vmem], out_specs=vm...  1.93 us
  transfers between devices with their start and end apart: 4, of which 3 were waited for; matrix products, arithmetic and copies ran while one was open for 0% of the time, Pallas kernels for 7%

profile of v5, /device:TPU:0, one launch (start us, length us, event | category | flops | bytes accessed | tf_op | source)
XLA Modules:
  0.0 73.1 jit_solution(2484635786688629621)
XLA Ops:
  0.6 0.6 collective-permute-start
  1.2 1.8 %overlap.1 = (f32[256,128]{1,0:T(8,128)S(1)}, bf16[256,768]{1,0:T(8,128)(2,1)S(1)}, bf16[256,768]{1,0:T(8,128)(2,1)S(1)}, bf16[768,256]{1,0:T(8,128)(2,1)S(1)}, ...) custom-call(f32[768,128]{1,0:T(8,128)} %bitcast.11, f32[768,256]{1,0:T(8,128)} %trial_ref.1), custom_call_target="tpu_custom_call" | custom-call | tf_op jit(solution)/shard_map/overlap/pallas_call | solution.py:451
  3.0 0.1 pad_add_fusion.core_ref
  3.1 0.0 collective-permute-done.other_ref
  3.1 7.2 %green.1 = (bf16[16,96,128]{2,1,0:T(8,128)(2,1)S(1)}, bf16[192,128,256]{2,1,0:T(8,128)(2,1)S(1)}) custom-call(s32[2]{0:T(128)S(1)} %pad_add_fusion.core_ref, f32[768,128]{1,0:T(8,128)S(1)} %collective-permute-done.other_ref, f32[256,128]{1,0:T(8,128)S(1)} %get-tuple-element.14.inter_ref, bf16[256,768]{1,0:T(8,128)(2,1)S(1)} %get-tuple-element.15.turned_high_ref, ...), custom_call_target="tpu_custom_call" | custom-call | tf_op jit(solution)/shard_map/green/pallas_call | solution.py:463
  10.3 0.0 copy-start.1
  10.3 20.9 %all_to_all.15.green_ref = bf16[16,96,128]{2,1,0:T(8,128)(2,1)S(1)} all-to-all(bf16[16,96,128]{2,1,0:T(8,128)(2,1)S(1)} %get-tuple-element.21), channel_id=1, replica_groups=mesh['groups'=1,'pairs'=4,'chol'=4,'walk'=2] {'pairs','chol'}, dimensions={0} | all-to-all | bytes 786432 | tf_op jit(solution)/shard_map/all_to_all | solution.py:482
  31.2 0.0 collective-permute-start.1
  31.2 0.9 %bias.2 = f32[1,16,256]{2,1,0:T(8,128)S(1)} custom-call(s32[1]{0:T(128)} %bitcast.place_ref.core_ref, bf16[16,96,128]{2,1,0:T(8,128)(2,1)S(1)} %all_to_all.15.green_ref, bf16[192,128,256]{2,1,0:T(8,128)(2,1)S(1)} %get-tuple-element.22.kept_ref, f32[16,256]{1,0:T(8,128)S(1)} %broadcast_in_dim.9.before_ref), custom_call_target="tpu_custom_call" | custom-call | tf_op jit(solution)/shard_map/bias/pallas_call | solution.py:405
  32.2 0.8 %collective-permute-done.1.green_ref = bf16[16,96,128]{2,1,0:T(8,128)(2,1)S(1)} collective-permute-done((bf16[16,96,128]{2,1,0:T(8,128)(2,1)S(1)}, bf16[16,96,128]{2,1,0:T(8,128)(2,1)S(1)}, u32[]{:S(2)}, u32[]{:S(2)}) %collective-permute-start.1) | collective-permute-done | bytes 393248 | tf_op jit(solution)/shard_map/ppermute | solution.py:25
  33.0 1.0 %bias.3 = f32[16,16,256]{2,1,0:T(8,128)S(1)} custom-call(s32[1]{0:T(128)S(6)} %sub.4.place_ref, bf16[16,96,128]{2,1,0:T(8,128)(2,1)S(1)} %collective-permute-done.1.green_ref, bf16[192,128,256]{2,1,0:T(8,128)(2,1)S(1)} %get-tuple-element.22.kept_ref, f32[16,256]{1,0:T(8,128)S(1)} %bitcast.15), custom_call_target="tpu_custom_call" | custom-call | tf_op jit(solution)/shard_map/bias/pallas_call | solution.py:405
  33.9 0.0 copy-start
  34.0 13.7 %all_to_all.16.parts_ref = f32[16,16,256]{2,1,0:T(8,128)S(1)} all-to-all(f32[16,16,256]{2,1,0:T(8,128)S(1)} %bias.3), channel_id=1, replica_groups=mesh['groups'=1,'pairs'=4,'chol'=4,'walk'=2] {'pairs','chol'}, dimensions={0} | all-to-all | bytes 524288 | tf_op jit(solution)/shard_map/all_to_all | solution.py:486
  47.7 0.0 copy-done.1
  47.7 1.9 %potential.3 = (f32[16,256]{1,0:T(8,128)}, f32[96,16,128]{2,1,0:T(8,128)S(1)}) custom-call(s32[1]{0:T(128)S(6)} %sub.4.place_ref, f32[16,16,256]{2,1,0:T(8,128)S(1)} %all_to_all.16.parts_ref, f32[16,256]{1,0:T(8,128)S(1)} %bitcast.13, bf16[192,128,256]{2,1,0:T(8,128)(2,1)S(1)} %get-tuple-element.22.kept_ref), custom_call_target="tpu_custom_call" | custom-call | tf_op jit(solution)/shard_map/potential/pallas_call | solution.py:426
  49.6 0.3 copy.6
  49.9 0.1 collective-permute-start.2
  49.9 1.9 %potential.2 = (f32[16,256]{1,0:T(8,128)}, f32[96,16,128]{2,1,0:T(8,128)S(1)}) custom-call(s32[1]{0:T(128)} %bitcast.place_ref.core_ref, f32[16,16,256]{2,1,0:T(8,128)S(1)} %all_to_all.16.parts_ref, f32[16,256]{1,0:T(8,128)S(1)} %bitcast.14, bf16[192,128,256]{2,1,0:T(8,128)(2,1)S(1)} %get-tuple-element.22.kept_ref), custom_call_target="tpu_custom_call" | custom-call | tf_op jit(solution)/shard_map/potential/pallas_call | solution.py:426
  51.8 0.4 collective-permute-done.2
  52.2 0.3 fusion.1
  52.5 16.2 %all_to_all.17.source_ref = bf16[16,96,128]{2,1,0:T(8,128)(2,1)S(1)} all-to-all(bf16[16,96,128]{2,1,0:T(8,128)(2,1)S(1)} %fusion.1), channel_id=1, replica_groups=mesh['groups'=1,'pairs'=4,'chol'=4,'walk'=2] {'pairs','chol'}, dimensions={0} | all-to-all | bytes 786432 | tf_op jit(solution)/shard_map/all_to_all | solution.py:490
  68.7 0.0 collective-permute-start.3
  68.7 0.1 joined.1.joined_ref
  68.9 1.6 %collective-permute-done.3.other_ref = bf16[16,96,128]{2,1,0:T(8,128)(2,1)S(1)} collective-permute-done((bf16[16,96,128]{2,1,0:T(8,128)(2,1)S(1)}, bf16[16,96,128]{2,1,0:T(8,128)(2,1)S(1)}, u32[]{:S(2)}, u32[]{:S(2)}) %collective-permute-start.3) | collective-permute-done | bytes 393248 | tf_op jit(solution)/shard_map/ppermute | solution.py:25
  70.5 0.0 copy-done
  70.5 2.7 %series.1 = f32[768,128]{1,0:T(8,128)} custom-call(s32[1]{0:T(128)} %bitcast.place_ref.core_ref, bf16[12,32,512]{2,1,0:T(8,128)(2,1)S(1)} %joined.1.joined_ref, bf16[16,96,128]{2,1,0:T(8,128)(2,1)S(1)} %collective-permute-done.3.other_ref, f32[768,128]{1,0:T(8,128)S(1)} %bitcast.12), custom_call_target="tpu_custom_call" | custom-call | tf_op jit(solution)/shard_map/series/pallas_call | solution.py:501
  (1 shorter events, 0.0 us)
Async XLA Ops:
  0.6 2.5 %collective-permute-start = (f32[768,128]{1,0:T(8,128)}, f32[768,128]{1,0:T(8,128)S(1)}, u32[]{:S(2)}, u32[]{:S(2)}) collective-permute-start(f32[768,128]{1,0:T(8,128)} %bitcast.10), channel_id=1, source_target_pairs={{0,1},{1,0},{2,3},{3,2},{4,5},{5,4},{6,7},{7,6},{8,9},{9,8},{10,11... | collective-permute-start | bytes 1179656 | tf_op jit(solution)/shard_map/ppermute | solution.py:25
  10.3 37.4 %copy-start.1 = (f32[1,16,256]{2,1,0:T(8,128)S(1)}, f32[1,16,256]{2,1,0:T(8,128)}, u32[]{:S(2)}) copy-start(f32[1,16,256]{2,1,0:T(8,128)} %param.7) | copy-start | bytes 49156
  31.2 1.7 %collective-permute-start.1 = (bf16[16,96,128]{2,1,0:T(8,128)(2,1)S(1)}, bf16[16,96,128]{2,1,0:T(8,128)(2,1)S(1)}, u32[]{:S(2)}, u32[]{:S(2)}) collective-permute-start(bf16[16,96,128]{2,1,0:T(8,128)(2,1)S(1)} %all_to_all.15.green_ref), channel_id=1, source_target_pairs={{0,1},{1,0},{2,3},{3,2},{4,5},{5,4},{6,7},{7,6},{8,9},{9,8},{10,11... | collective-permute-start | bytes 1179656 | tf_op jit(solution)/shard_map/ppermute | solution.py:25
  33.9 36.5 %copy-start = (f32[1,768,128]{2,1,0:T(8,128)S(1)}, f32[1,768,128]{2,1,0:T(8,128)}, u32[]{:S(2)}) copy-start(f32[1,768,128]{2,1,0:T(8,128)} %param.6) | copy-start | bytes 1179652
  49.9 2.4 %collective-permute-start.2 = (f32[96,16,128]{2,0,1:T(8,128)S(1)}, f32[96,16,128]{2,0,1:T(8,128)S(1)}, u32[]{:S(2)}, u32[]{:S(2)}) collective-permute-start(f32[96,16,128]{2,0,1:T(8,128)S(1)} %copy.6), channel_id=1, source_target_pairs={{0,1},{1,0},{2,3},{3,2},{4,5},{5,4},{6,7},{7,6},{8,9},{9,8},{10,11... | collective-permute-start | bytes 2359304 | tf_op jit(solution)/shard_map/ppermute | solution.py:25
  68.7 1.7 %collective-permute-start.3 = (bf16[16,96,128]{2,1,0:T(8,128)(2,1)S(1)}, bf16[16,96,128]{2,1,0:T(8,128)(2,1)S(1)}, u32[]{:S(2)}, u32[]{:S(2)}) collective-permute-start(bf16[16,96,128]{2,1,0:T(8,128)(2,1)S(1)} %all_to_all.17.source_ref), channel_id=1, source_target_pairs={{0,1},{1,0},{2,3},{3,2},{4,5},{5,4},{6,7},{7,6},{8,9},{9,8},{10,11... | collective-permute-start | bytes 1179656 | tf_op jit(solution)/shard_map/ppermute | solution.py:25

commit v6 on v5

--- a/solution.py
+++ b/solution.py
@@ -331,13 +331,21 @@
     return jnp.concatenate(same + beside, axis=1)
 
 
-def joined_body(source_ref, out_ref, *, row_groups, col_groups):
+def joined_body(source_ref, walker_ref, out_ref, turned_ref, pair_ref, *, row_groups, col_groups):
     for sub in range(SUBS):
         for row in range(row_groups):
             out_ref[sub * row_groups + row] = joined_tiles(source_ref, sub, row, col_groups)
-
-
-def series_body(core_ref, joined_ref, other_ref, walker_ref, out_ref, matrix_ref, stage_ref, sems, *, row_groups, col_groups):
+    slab = SUB * SUBS
+    pieces = []
+    for sub in range(SUBS):
+        for row in range(row_groups):
+            pieces.append(walker_ref[row * slab + sub * SUB : row * slab + (sub + 1) * SUB, :])
+    term = jnp.concatenate(pieces, axis=0).T
+    turned_ref[...] = term
+    pair_ref[...] = jnp.concatenate(split_two(term), axis=0)
+
+
+def series_body(core_ref, joined_ref, turned_ref, pair_ref, other_ref, out_ref, matrix_ref, stage_ref, sems, *, row_groups, col_groups):
     slab = SUB * SUBS
     part = SUB // 2
     size = row_groups * SUB
@@ -360,22 +368,16 @@
         block = matrix_ref[sub * size : (sub + 1) * size, following * size : (following + 1) * size]
         matrix_ref[following * size : (following + 1) * size, sub * size : (sub + 1) * size] = block.T
 
-    pieces = []
-    for sub in range(SUBS):
-        for row in range(row_groups):
-            pieces.append(walker_ref[row * slab + sub * SUB : row * slab + (sub + 1) * SUB, :])
-    term = jnp.concatenate(pieces, axis=0).T
-    total = term
-    count = term.shape[0]
+    total = turned_ref[...]
+    count = total.shape[0]
+    left = pair_ref[...]
     for degree in range(1, TERMS):
-        pair = split_two(term)
+        both = dot_of(left, matrix_ref[...])
         if degree < 3:
-            both = dot_of(jnp.concatenate(pair, axis=0), matrix_ref[...])
             both = both[:count] + both[count:]
-        else:
-            both = dot_of(pair[0], matrix_ref[...])
         term = (-root_step / degree) * both
         total = total + term
+        left = jnp.concatenate(split_two(term), axis=0) if degree == 1 else term.astype(bf16)
     copies = []
     for sub in range(SUBS):
         rows = slice(sub * size, (sub + 1) * size)
@@ -490,18 +492,23 @@
     received = lax.all_to_all(summed, axes, split_axis=0, concat_axis=0, tiled=True)
     received_other = swapped(received, "walk", 0)
     sizes = dict(row_groups=row_groups, col_groups=col_groups)
-    joined = pl.pallas_call(
+    width = own.shape[1]
+    prepared = pl.pallas_call(
         functools.partial(joined_body, **sizes),
-        out_shape=jax.ShapeDtypeStruct((SUBS * row_groups, SUB // 2, 2 * SUB * col_groups), bf16),
-        in_specs=[vmem],
-        out_specs=vmem,
+        out_shape=(
+            jax.ShapeDtypeStruct((SUBS * row_groups, SUB // 2, 2 * SUB * col_groups), bf16),
+            jax.ShapeDtypeStruct((width, orbital_count), f32),
+            jax.ShapeDtypeStruct((2 * width, orbital_count), bf16),
+        ),
+        in_specs=[vmem, vmem],
+        out_specs=(vmem, vmem, vmem),
         compiler_params=grant,
         name="joined",
-    )(received)
+    )(received, own)
     propagated = pl.pallas_call(
         functools.partial(series_body, **sizes),
         out_shape=jax.ShapeDtypeStruct(own.shape, f32),
-        in_specs=[smem, vmem, vmem, vmem],
+        in_specs=[smem, vmem, vmem, vmem, vmem],
         out_specs=anywhere,
         scratch_shapes=[
             pltpu.VMEM((orbital_count, orbital_count), bf16),
@@ -510,7 +517,7 @@
         ],
         compiler_params=grant,
         name="series",
-    )(core, joined, received_other, own)
+    )(core, *prepared, received_other)
     return propagated[None], force_bias[None]
 
 

time: 73.4 us -> 73.3 us (level)
  no operation moved by 1% of the time
where the time goes in v6:
time: 73.3 us; the launch traced here: 73 us
  blocking collectives  50.8 us (69%)
  Pallas kernels  17.5 us (24%)
  waiting for transfers between devices  2.62 us (4%)
    all_to_all x1, blocking collectives, fast_shards(): lax.all_to_all(outgoing, axes, split_axis=0, concat_axis=0, tiled=True)  20.9 us
    all_to_all x1, blocking collectives, fast_shards(): lax.all_to_all(summed, axes, split_axis=0, concat_axis=0, tiled=True)  16.2 us
    all_to_all x1, blocking collectives, fast_shards(): lax.all_to_all(spread, axes, split_axis=0, concat_axis=0, tiled=True)  13.6 us
    pallas_call x1, Pallas kernels, fast_shards(): pl.pallas_call(functools.partial(green_body, row_groups=row_groups, col_g...  7.21 us
    pallas_call x2, Pallas kernels, potential_half(): pl.pallas_call(potential_body, in_specs=[smem, vmem, vmem, vmem], out_spe...  3.78 us
    ppermute x4, waiting for transfers between devices, swapped(): return lax.ppermute(value, axis, pairs)  2.62 us
    pallas_call x1, Pallas kernels, fast_shards(): pl.pallas_call(functools.partial(series_body, **sizes), out_shape=jax.Sha...  2.58 us
    pallas_call x2, Pallas kernels, bias_half(): pl.pallas_call(bias_body, in_specs=[smem, vmem, vmem, vmem], out_specs=vm...  1.93 us
  transfers between devices with their start and end apart: 4, of which 3 were waited for; matrix products, arithmetic and copies ran while one was open for 0% of the time, Pallas kernels for 7%

profile of v6, /device:TPU:0, one launch (start us, length us, event | category | flops | bytes accessed | tf_op | source)
XLA Modules:
  0.0 73.0 jit_solution(17026942974636221014)
XLA Ops:
  0.6 0.6 collective-permute-start
  1.2 1.8 %overlap.1 = (f32[256,128]{1,0:T(8,128)S(1)}, bf16[256,768]{1,0:T(8,128)(2,1)S(1)}, bf16[256,768]{1,0:T(8,128)(2,1)S(1)}, bf16[768,256]{1,0:T(8,128)(2,1)S(1)}, ...) custom-call(f32[768,128]{1,0:T(8,128)} %bitcast.11, f32[768,256]{1,0:T(8,128)} %trial_ref.1), custom_call_target="tpu_custom_call" | custom-call | tf_op jit(solution)/shard_map/overlap/pallas_call | solution.py:453
  3.0 0.1 pad_add_fusion.core_ref
  3.1 0.0 collective-permute-done.other_ref
  3.1 7.2 %green.1 = (bf16[16,96,128]{2,1,0:T(8,128)(2,1)S(1)}, bf16[192,128,256]{2,1,0:T(8,128)(2,1)S(1)}) custom-call(s32[2]{0:T(128)S(1)} %pad_add_fusion.core_ref, f32[768,128]{1,0:T(8,128)S(1)} %collective-permute-done.other_ref, f32[256,128]{1,0:T(8,128)S(1)} %get-tuple-element.17.inter_ref, bf16[256,768]{1,0:T(8,128)(2,1)S(1)} %get-tuple-element.18.turned_high_ref, ...), custom_call_target="tpu_custom_call" | custom-call | tf_op jit(solution)/shard_map/green/pallas_call | solution.py:465
  10.3 0.0 copy-start.1
  10.3 20.9 %all_to_all.15.green_ref = bf16[16,96,128]{2,1,0:T(8,128)(2,1)S(1)} all-to-all(bf16[16,96,128]{2,1,0:T(8,128)(2,1)S(1)} %get-tuple-element.24), channel_id=1, replica_groups=mesh['groups'=1,'pairs'=4,'chol'=4,'walk'=2] {'pairs','chol'}, dimensions={0} | all-to-all | bytes 786432 | tf_op jit(solution)/shard_map/all_to_all | solution.py:484
  31.2 0.0 collective-permute-start.1
  31.2 0.9 %bias.2 = f32[1,16,256]{2,1,0:T(8,128)S(1)} custom-call(s32[1]{0:T(128)} %bitcast.place_ref.core_ref, bf16[16,96,128]{2,1,0:T(8,128)(2,1)S(1)} %all_to_all.15.green_ref, bf16[192,128,256]{2,1,0:T(8,128)(2,1)S(1)} %get-tuple-element.25.kept_ref, f32[16,256]{1,0:T(8,128)S(1)} %broadcast_in_dim.9.before_ref), custom_call_target="tpu_custom_call" | custom-call | tf_op jit(solution)/shard_map/bias/pallas_call | solution.py:407
  32.2 0.8 %collective-permute-done.1.green_ref = bf16[16,96,128]{2,1,0:T(8,128)(2,1)S(1)} collective-permute-done((bf16[16,96,128]{2,1,0:T(8,128)(2,1)S(1)}, bf16[16,96,128]{2,1,0:T(8,128)(2,1)S(1)}, u32[]{:S(2)}, u32[]{:S(2)}) %collective-permute-start.1) | collective-permute-done | bytes 393248 | tf_op jit(solution)/shard_map/ppermute | solution.py:25
  33.0 0.0 copy-start
  33.0 1.0 %bias.3 = f32[16,16,256]{2,1,0:T(8,128)S(1)} custom-call(s32[1]{0:T(128)S(6)} %sub.4.place_ref, bf16[16,96,128]{2,1,0:T(8,128)(2,1)S(1)} %collective-permute-done.1.green_ref, bf16[192,128,256]{2,1,0:T(8,128)(2,1)S(1)} %get-tuple-element.25.kept_ref, f32[16,256]{1,0:T(8,128)S(1)} %bitcast.15), custom_call_target="tpu_custom_call" | custom-call | tf_op jit(solution)/shard_map/bias/pallas_call | solution.py:407
  33.9 13.6 %all_to_all.16.parts_ref = f32[16,16,256]{2,1,0:T(8,128)S(1)} all-to-all(f32[16,16,256]{2,1,0:T(8,128)S(1)} %bias.3), channel_id=1, replica_groups=mesh['groups'=1,'pairs'=4,'chol'=4,'walk'=2] {'pairs','chol'}, dimensions={0} | all-to-all | bytes 524288 | tf_op jit(solution)/shard_map/all_to_all | solution.py:488
  47.6 0.0 copy-done.1
  47.6 1.9 %potential.3 = (f32[16,256]{1,0:T(8,128)}, f32[96,16,128]{2,1,0:T(8,128)S(1)}) custom-call(s32[1]{0:T(128)S(6)} %sub.4.place_ref, f32[16,16,256]{2,1,0:T(8,128)S(1)} %all_to_all.16.parts_ref, f32[16,256]{1,0:T(8,128)S(1)} %bitcast.13, bf16[192,128,256]{2,1,0:T(8,128)(2,1)S(1)} %get-tuple-element.25.kept_ref), custom_call_target="tpu_custom_call" | custom-call | tf_op jit(solution)/shard_map/potential/pallas_call | solution.py:428
  49.4 0.3 copy.6
  49.7 0.1 collective-permute-start.2
  49.8 1.9 %potential.2 = (f32[16,256]{1,0:T(8,128)}, f32[96,16,128]{2,1,0:T(8,128)S(1)}) custom-call(s32[1]{0:T(128)} %bitcast.place_ref.core_ref, f32[16,16,256]{2,1,0:T(8,128)S(1)} %all_to_all.16.parts_ref, f32[16,256]{1,0:T(8,128)S(1)} %bitcast.14, bf16[192,128,256]{2,1,0:T(8,128)(2,1)S(1)} %get-tuple-element.25.kept_ref), custom_call_target="tpu_custom_call" | custom-call | tf_op jit(solution)/shard_map/potential/pallas_call | solution.py:428
  51.7 0.4 collective-permute-done.2
  52.1 0.4 fusion.1
  52.4 16.2 %all_to_all.17.source_ref = bf16[16,96,128]{2,1,0:T(8,128)(2,1)S(1)} all-to-all(bf16[16,96,128]{2,1,0:T(8,128)(2,1)S(1)} %fusion.1), channel_id=1, replica_groups=mesh['groups'=1,'pairs'=4,'chol'=4,'walk'=2] {'pairs','chol'}, dimensions={0} | all-to-all | bytes 786432 | tf_op jit(solution)/shard_map/all_to_all | solution.py:492
  68.7 0.0 collective-permute-start.3
  68.7 0.0 copy-done
  68.7 0.2 joined.1
  68.9 1.5 %collective-permute-done.3.other_ref = bf16[16,96,128]{2,1,0:T(8,128)(2,1)S(1)} collective-permute-done((bf16[16,96,128]{2,1,0:T(8,128)(2,1)S(1)}, bf16[16,96,128]{2,1,0:T(8,128)(2,1)S(1)}, u32[]{:S(2)}, u32[]{:S(2)}) %collective-permute-start.3) | collective-permute-done | bytes 393248 | tf_op jit(solution)/shard_map/ppermute | solution.py:25
  70.4 2.6 %series.1 = f32[768,128]{1,0:T(8,128)} custom-call(s32[1]{0:T(128)} %bitcast.place_ref.core_ref, bf16[12,32,512]{2,1,0:T(8,128)(2,1)S(1)} %get-tuple-element.28.joined_ref, f32[128,768]{1,0:T(8,128)S(1)} %get-tuple-element.29.turned_ref, bf16[256,768]{1,0:T(8,128)(2,1)S(1)} %get-tuple-element.30.pair_ref, ...), custom_call_target="tpu_custom_call" | custom-call | tf_op jit(solution)/shard_map/series/pallas_call | solution.py:508
  (1 shorter events, 0.0 us)
Async XLA Ops:
  0.6 2.5 %collective-permute-start = (f32[768,128]{1,0:T(8,128)}, f32[768,128]{1,0:T(8,128)S(1)}, u32[]{:S(2)}, u32[]{:S(2)}) collective-permute-start(f32[768,128]{1,0:T(8,128)} %bitcast.10), channel_id=1, source_target_pairs={{0,1},{1,0},{2,3},{3,2},{4,5},{5,4},{6,7},{7,6},{8,9},{9,8},{10,11... | collective-permute-start | bytes 1179656 | tf_op jit(solution)/shard_map/ppermute | solution.py:25
  10.3 37.3 %copy-start.1 = (f32[1,16,256]{2,1,0:T(8,128)S(1)}, f32[1,16,256]{2,1,0:T(8,128)}, u32[]{:S(2)}) copy-start(f32[1,16,256]{2,1,0:T(8,128)} %param.7) | copy-start | bytes 49156
  31.2 1.7 %collective-permute-start.1 = (bf16[16,96,128]{2,1,0:T(8,128)(2,1)S(1)}, bf16[16,96,128]{2,1,0:T(8,128)(2,1)S(1)}, u32[]{:S(2)}, u32[]{:S(2)}) collective-permute-start(bf16[16,96,128]{2,1,0:T(8,128)(2,1)S(1)} %all_to_all.15.green_ref), channel_id=1, source_target_pairs={{0,1},{1,0},{2,3},{3,2},{4,5},{5,4},{6,7},{7,6},{8,9},{9,8},{10,11... | collective-permute-start | bytes 1179656 | tf_op jit(solution)/shard_map/ppermute | solution.py:25
  33.0 35.7 %copy-start = (f32[1,768,128]{2,1,0:T(8,128)S(1)}, f32[1,768,128]{2,1,0:T(8,128)}, u32[]{:S(2)}) copy-start(f32[1,768,128]{2,1,0:T(8,128)} %param.6) | copy-start | bytes 1179652
  49.7 2.4 %collective-permute-start.2 = (f32[96,16,128]{2,0,1:T(8,128)S(1)}, f32[96,16,128]{2,0,1:T(8,128)S(1)}, u32[]{:S(2)}, u32[]{:S(2)}) collective-permute-start(f32[96,16,128]{2,0,1:T(8,128)S(1)} %copy.6), channel_id=1, source_target_pairs={{0,1},{1,0},{2,3},{3,2},{4,5},{5,4},{6,7},{7,6},{8,9},{9,8},{10,11... | collective-permute-start | bytes 2359304 | tf_op jit(solution)/shard_map/ppermute | solution.py:25
  68.7 1.7 %collective-permute-start.3 = (bf16[16,96,128]{2,1,0:T(8,128)(2,1)S(1)}, bf16[16,96,128]{2,1,0:T(8,128)(2,1)S(1)}, u32[]{:S(2)}, u32[]{:S(2)}) collective-permute-start(bf16[16,96,128]{2,1,0:T(8,128)(2,1)S(1)} %all_to_all.17.source_ref), channel_id=1, source_target_pairs={{0,1},{1,0},{2,3},{3,2},{4,5},{5,4},{6,7},{7,6},{8,9},{9,8},{10,11... | collective-permute-start | bytes 1179656 | tf_op jit(solution)/shard_map/ppermute | solution.py:25

commit v7 on v6

--- a/solution.py
+++ b/solution.py
@@ -373,11 +373,11 @@
     left = pair_ref[...]
     for degree in range(1, TERMS):
         both = dot_of(left, matrix_ref[...])
-        if degree < 3:
+        if degree < 2:
             both = both[:count] + both[count:]
         term = (-root_step / degree) * both
         total = total + term
-        left = jnp.concatenate(split_two(term), axis=0) if degree == 1 else term.astype(bf16)
+        left = term.astype(bf16)
     copies = []
     for sub in range(SUBS):
         rows = slice(sub * size, (sub + 1) * size)

time: 73.3 us -> 73.2 us (level)
  no operation moved by 1% of the time
where the time goes in v7:
time: 73.2 us; the launch traced here: 72.9 us
  blocking collectives  50.8 us (69%)
  Pallas kernels  17.5 us (24%)
  waiting for transfers between devices  2.62 us (4%)
    all_to_all x1, blocking collectives, fast_shards(): lax.all_to_all(outgoing, axes, split_axis=0, concat_axis=0, tiled=True)  20.9 us
    all_to_all x1, blocking collectives, fast_shards(): lax.all_to_all(summed, axes, split_axis=0, concat_axis=0, tiled=True)  16.2 us
    all_to_all x1, blocking collectives, fast_shards(): lax.all_to_all(spread, axes, split_axis=0, concat_axis=0, tiled=True)  13.6 us
    pallas_call x1, Pallas kernels, fast_shards(): pl.pallas_call(functools.partial(green_body, row_groups=row_groups, col_g...  7.21 us
    pallas_call x2, Pallas kernels, potential_half(): pl.pallas_call(potential_body, in_specs=[smem, vmem, vmem, vmem], out_spe...  3.78 us
    ppermute x4, waiting for transfers between devices, swapped(): return lax.ppermute(value, axis, pairs)  2.62 us
    pallas_call x1, Pallas kernels, fast_shards(): pl.pallas_call(functools.partial(series_body, **sizes), out_shape=jax.Sha...  2.55 us
    pallas_call x2, Pallas kernels, bias_half(): pl.pallas_call(bias_body, in_specs=[smem, vmem, vmem, vmem], out_specs=vm...  1.93 us
  transfers between devices with their start and end apart: 4, of which 3 were waited for; matrix products, arithmetic and copies ran while one was open for 0% of the time, Pallas kernels for 7%

profile of v7, /device:TPU:0, one launch (start us, length us, event | category | flops | bytes accessed | tf_op | source)
XLA Modules:
  0.0 72.9 jit_solution(7329384412856983790)
XLA Ops:
  0.6 0.6 collective-permute-start
  1.2 1.8 %overlap.1 = (f32[256,128]{1,0:T(8,128)S(1)}, bf16[256,768]{1,0:T(8,128)(2,1)S(1)}, bf16[256,768]{1,0:T(8,128)(2,1)S(1)}, bf16[768,256]{1,0:T(8,128)(2,1)S(1)}, ...) custom-call(f32[768,128]{1,0:T(8,128)} %bitcast.11, f32[768,256]{1,0:T(8,128)} %trial_ref.1), custom_call_target="tpu_custom_call" | custom-call | tf_op jit(solution)/shard_map/overlap/pallas_call | solution.py:453
  3.0 0.1 pad_add_fusion.core_ref
  3.1 0.0 collective-permute-done.other_ref
  3.1 7.2 %green.1 = (bf16[16,96,128]{2,1,0:T(8,128)(2,1)S(1)}, bf16[192,128,256]{2,1,0:T(8,128)(2,1)S(1)}) custom-call(s32[2]{0:T(128)S(1)} %pad_add_fusion.core_ref, f32[768,128]{1,0:T(8,128)S(1)} %collective-permute-done.other_ref, f32[256,128]{1,0:T(8,128)S(1)} %get-tuple-element.17.inter_ref, bf16[256,768]{1,0:T(8,128)(2,1)S(1)} %get-tuple-element.18.turned_high_ref, ...), custom_call_target="tpu_custom_call" | custom-call | tf_op jit(solution)/shard_map/green/pallas_call | solution.py:465
  10.3 0.0 copy-start.1
  10.3 20.9 %all_to_all.15.green_ref = bf16[16,96,128]{2,1,0:T(8,128)(2,1)S(1)} all-to-all(bf16[16,96,128]{2,1,0:T(8,128)(2,1)S(1)} %get-tuple-element.24), channel_id=1, replica_groups=mesh['groups'=1,'pairs'=4,'chol'=4,'walk'=2] {'pairs','chol'}, dimensions={0} | all-to-all | bytes 786432 | tf_op jit(solution)/shard_map/all_to_all | solution.py:484
  31.2 0.0 collective-permute-start.1
  31.2 0.9 %bias.2 = f32[1,16,256]{2,1,0:T(8,128)S(1)} custom-call(s32[1]{0:T(128)} %bitcast.place_ref.core_ref, bf16[16,96,128]{2,1,0:T(8,128)(2,1)S(1)} %all_to_all.15.green_ref, bf16[192,128,256]{2,1,0:T(8,128)(2,1)S(1)} %get-tuple-element.25.kept_ref, f32[16,256]{1,0:T(8,128)S(1)} %broadcast_in_dim.9.before_ref), custom_call_target="tpu_custom_call" | custom-call | tf_op jit(solution)/shard_map/bias/pallas_call | solution.py:407
  32.2 0.8 %collective-permute-done.1.green_ref = bf16[16,96,128]{2,1,0:T(8,128)(2,1)S(1)} collective-permute-done((bf16[16,96,128]{2,1,0:T(8,128)(2,1)S(1)}, bf16[16,96,128]{2,1,0:T(8,128)(2,1)S(1)}, u32[]{:S(2)}, u32[]{:S(2)}) %collective-permute-start.1) | collective-permute-done | bytes 393248 | tf_op jit(solution)/shard_map/ppermute | solution.py:25
  33.0 0.0 copy-start
  33.0 1.0 %bias.3 = f32[16,16,256]{2,1,0:T(8,128)S(1)} custom-call(s32[1]{0:T(128)S(6)} %sub.4.place_ref, bf16[16,96,128]{2,1,0:T(8,128)(2,1)S(1)} %collective-permute-done.1.green_ref, bf16[192,128,256]{2,1,0:T(8,128)(2,1)S(1)} %get-tuple-element.25.kept_ref, f32[16,256]{1,0:T(8,128)S(1)} %bitcast.15), custom_call_target="tpu_custom_call" | custom-call | tf_op jit(solution)/shard_map/bias/pallas_call | solution.py:407
  33.9 13.6 %all_to_all.16.parts_ref = f32[16,16,256]{2,1,0:T(8,128)S(1)} all-to-all(f32[16,16,256]{2,1,0:T(8,128)S(1)} %bias.3), channel_id=1, replica_groups=mesh['groups'=1,'pairs'=4,'chol'=4,'walk'=2] {'pairs','chol'}, dimensions={0} | all-to-all | bytes 524288 | tf_op jit(solution)/shard_map/all_to_all | solution.py:488
  47.6 0.0 copy-done.1
  47.6 1.9 %potential.3 = (f32[16,256]{1,0:T(8,128)}, f32[96,16,128]{2,1,0:T(8,128)S(1)}) custom-call(s32[1]{0:T(128)S(6)} %sub.4.place_ref, f32[16,16,256]{2,1,0:T(8,128)S(1)} %all_to_all.16.parts_ref, f32[16,256]{1,0:T(8,128)S(1)} %bitcast.13, bf16[192,128,256]{2,1,0:T(8,128)(2,1)S(1)} %get-tuple-element.25.kept_ref), custom_call_target="tpu_custom_call" | custom-call | tf_op jit(solution)/shard_map/potential/pallas_call | solution.py:428
  49.4 0.3 copy.6
  49.7 0.1 collective-permute-start.2
  49.8 1.9 %potential.2 = (f32[16,256]{1,0:T(8,128)}, f32[96,16,128]{2,1,0:T(8,128)S(1)}) custom-call(s32[1]{0:T(128)} %bitcast.place_ref.core_ref, f32[16,16,256]{2,1,0:T(8,128)S(1)} %all_to_all.16.parts_ref, f32[16,256]{1,0:T(8,128)S(1)} %bitcast.14, bf16[192,128,256]{2,1,0:T(8,128)(2,1)S(1)} %get-tuple-element.25.kept_ref), custom_call_target="tpu_custom_call" | custom-call | tf_op jit(solution)/shard_map/potential/pallas_call | solution.py:428
  51.7 0.4 collective-permute-done.2
  52.1 0.4 fusion.1
  52.4 16.2 %all_to_all.17.source_ref = bf16[16,96,128]{2,1,0:T(8,128)(2,1)S(1)} all-to-all(bf16[16,96,128]{2,1,0:T(8,128)(2,1)S(1)} %fusion.1), channel_id=1, replica_groups=mesh['groups'=1,'pairs'=4,'chol'=4,'walk'=2] {'pairs','chol'}, dimensions={0} | all-to-all | bytes 786432 | tf_op jit(solution)/shard_map/all_to_all | solution.py:492
  68.7 0.0 collective-permute-start.3
  68.7 0.0 copy-done
  68.7 0.2 joined.1
  68.9 1.5 %collective-permute-done.3.other_ref = bf16[16,96,128]{2,1,0:T(8,128)(2,1)S(1)} collective-permute-done((bf16[16,96,128]{2,1,0:T(8,128)(2,1)S(1)}, bf16[16,96,128]{2,1,0:T(8,128)(2,1)S(1)}, u32[]{:S(2)}, u32[]{:S(2)}) %collective-permute-start.3) | collective-permute-done | bytes 393248 | tf_op jit(solution)/shard_map/ppermute | solution.py:25
  70.4 2.5 %series.1 = f32[768,128]{1,0:T(8,128)} custom-call(s32[1]{0:T(128)} %bitcast.place_ref.core_ref, bf16[12,32,512]{2,1,0:T(8,128)(2,1)S(1)} %get-tuple-element.28.joined_ref, f32[128,768]{1,0:T(8,128)S(1)} %get-tuple-element.29.turned_ref, bf16[256,768]{1,0:T(8,128)(2,1)S(1)} %get-tuple-element.30.pair_ref, ...), custom_call_target="tpu_custom_call" | custom-call | tf_op jit(solution)/shard_map/series/pallas_call | solution.py:508
  (1 shorter events, 0.0 us)
Async XLA Ops:
  0.6 2.5 %collective-permute-start = (f32[768,128]{1,0:T(8,128)}, f32[768,128]{1,0:T(8,128)S(1)}, u32[]{:S(2)}, u32[]{:S(2)}) collective-permute-start(f32[768,128]{1,0:T(8,128)} %bitcast.10), channel_id=1, source_target_pairs={{0,1},{1,0},{2,3},{3,2},{4,5},{5,4},{6,7},{7,6},{8,9},{9,8},{10,11... | collective-permute-start | bytes 1179656 | tf_op jit(solution)/shard_map/ppermute | solution.py:25
  10.3 37.3 %copy-start.1 = (f32[1,16,256]{2,1,0:T(8,128)S(1)}, f32[1,16,256]{2,1,0:T(8,128)}, u32[]{:S(2)}) copy-start(f32[1,16,256]{2,1,0:T(8,128)} %param.7) | copy-start | bytes 49156
  31.2 1.7 %collective-permute-start.1 = (bf16[16,96,128]{2,1,0:T(8,128)(2,1)S(1)}, bf16[16,96,128]{2,1,0:T(8,128)(2,1)S(1)}, u32[]{:S(2)}, u32[]{:S(2)}) collective-permute-start(bf16[16,96,128]{2,1,0:T(8,128)(2,1)S(1)} %all_to_all.15.green_ref), channel_id=1, source_target_pairs={{0,1},{1,0},{2,3},{3,2},{4,5},{5,4},{6,7},{7,6},{8,9},{9,8},{10,11... | collective-permute-start | bytes 1179656 | tf_op jit(solution)/shard_map/ppermute | solution.py:25
  33.0 35.7 %copy-start = (f32[1,768,128]{2,1,0:T(8,128)S(1)}, f32[1,768,128]{2,1,0:T(8,128)}, u32[]{:S(2)}) copy-start(f32[1,768,128]{2,1,0:T(8,128)} %param.6) | copy-start | bytes 1179652
  49.7 2.4 %collective-permute-start.2 = (f32[96,16,128]{2,0,1:T(8,128)S(1)}, f32[96,16,128]{2,0,1:T(8,128)S(1)}, u32[]{:S(2)}, u32[]{:S(2)}) collective-permute-start(f32[96,16,128]{2,0,1:T(8,128)S(1)} %copy.6), channel_id=1, source_target_pairs={{0,1},{1,0},{2,3},{3,2},{4,5},{5,4},{6,7},{7,6},{8,9},{9,8},{10,11... | collective-permute-start | bytes 2359304 | tf_op jit(solution)/shard_map/ppermute | solution.py:25
  68.7 1.7 %collective-permute-start.3 = (bf16[16,96,128]{2,1,0:T(8,128)(2,1)S(1)}, bf16[16,96,128]{2,1,0:T(8,128)(2,1)S(1)}, u32[]{:S(2)}, u32[]{:S(2)}) collective-permute-start(bf16[16,96,128]{2,1,0:T(8,128)(2,1)S(1)} %all_to_all.17.source_ref), channel_id=1, source_target_pairs={{0,1},{1,0},{2,3},{3,2},{4,5},{5,4},{6,7},{7,6},{8,9},{9,8},{10,11... | collective-permute-start | bytes 1179656 | tf_op jit(solution)/shard_map/ppermute | solution.py:25
